TPU v7x, 32 devices: a whole 2x2x4 slice. The times are simulated.
32 devices in a mesh: row: 8 (over y, x, core), col: 4 (over z).
Axes of the slice: x: 2, y: 2, z: 4, core: 2. Of those that a mesh axis runs over, the one named last changes fastest.
Arguments:
- pair_map: float32 [128, 8192], P('row', 'col'), may hold values from -40 to 40
- cotangent: float32 [128, 8192], P('row', 'col'), may hold values from -50 to 50
- conv_one: float32 [3, 3, 64, 64], replicated, may hold values from -0.25 to 0.25
- conv_two: float32 [3, 3, 64, 64], replicated, may hold values from -0.25 to 0.25
- norm_gain: float32 [2, 64], replicated, may hold values from 0.5 to 2
- norm_shift: float32 [2, 64], replicated, may hold values from -2 to 2
Outputs:
- sym_out: float32 [128, 8192], P('row', 'col')
- grad_map: float32 [128, 8192], P('row', 'col')
- grad_one: float32 [3, 3, 64, 64], replicated
- grad_two: float32 [3, 3, 64, 64], replicated
- grad_gain: float32 [2, 64], replicated
- grad_shift: float32 [2, 64], replicated
All inputs are finite; a program needn't handle non-finite values.
Results may differ from a plain program's by a relative error of at most 0.000086.
Values sent between devices are 32-bit elements; how exact they have to be, the bound alone decides.
No kernel may reach another device: no remote copies, remote signals or barrier semaphores. Data moves between devices by JAX's collectives and lax.ppermute only.
A program may use at most 64 MiB of HBM per device.

v0:
```python
import jax
import jax.numpy as jnp
from jax import lax
from jax.sharding import PartitionSpec as P

DILATION_STEP = 16


epsilon = 1e-05
highest = lax.Precision.HIGHEST


def extended_2(cells, sides, width):
    for axis, dim in sides:
        count = lax.axis_size(axis)
        ends = count - 1
        head = lax.slice_in_dim(cells, 0, width, axis=dim)
        tail = lax.slice_in_dim(cells, cells.shape[dim] - width, cells.shape[dim], axis=dim)
        cells = jnp.concatenate(
            [
                lax.ppermute(tail, axis, [(i, (i + 1) % count) for i in range(ends)]),
                cells,
                lax.ppermute(head, axis, [((i + 1) % count, i) for i in range(ends)]),
            ],
            axis=dim,
        )
    return cells


def extend(feature_field_patch):
    block_result = extended_2(feature_field_patch, (("row", 0), ("col", 1)), DILATION_STEP)
    return block_result


def tap_windows(extended, row_begin, column_starts, local_row_count, local_column_count):
    pieces = [
        extended[row_begin : row_begin + local_row_count, start : start + local_column_count]
        for start in column_starts
    ]
    joined = jnp.concatenate(pieces, axis=2)
    return joined.reshape(local_row_count * local_column_count, -1)


def dilated(extended, filter_weight, local_row_count, local_column_count):
    channels = filter_weight.shape[2]
    starts = [tap * DILATION_STEP for tap in range(3)]
    summed_taps = jnp.zeros(
        (local_row_count * local_column_count, filter_weight.shape[3]), jnp.float32
    )
    for filter_tap_row in range(3):
        window = tap_windows(
            extended, filter_tap_row * DILATION_STEP, starts, local_row_count, local_column_count
        )
        stacked = filter_weight[filter_tap_row].reshape(3 * channels, -1)
        summed_taps = summed_taps + jnp.dot(
            window, stacked, precision=highest, preferred_element_type=jnp.float32
        )
    return summed_taps.reshape(local_row_count, local_column_count, -1)


def dilated_back(grad_ext, filter_weight, local_row_count, local_column_count):
    channels = filter_weight.shape[3]
    starts = [(2 - tap) * DILATION_STEP for tap in range(3)]
    summed_taps = jnp.zeros(
        (local_row_count * local_column_count, filter_weight.shape[2]), jnp.float32
    )
    for filter_tap_row in range(3):
        window = tap_windows(
            grad_ext,
            (2 - filter_tap_row) * DILATION_STEP,
            starts,
            local_row_count,
            local_column_count,
        )
        stacked = jnp.transpose(filter_weight[filter_tap_row], (0, 2, 1)).reshape(3 * channels, -1)
        summed_taps = summed_taps + jnp.dot(
            window, stacked, precision=highest, preferred_element_type=jnp.float32
        )
    return summed_taps.reshape(local_row_count, local_column_count, -1)


def kernel_grad(extended, grad_tile, local_row_count, local_column_count):
    channels = extended.shape[2]
    starts = [tap * DILATION_STEP for tap in range(3)]
    grad_flat = grad_tile.reshape(-1, grad_tile.shape[2])
    tap_list = []
    for filter_tap_row in range(3):
        window = tap_windows(
            extended, filter_tap_row * DILATION_STEP, starts, local_row_count, local_column_count
        )
        product = lax.dot_general(
            window,
            grad_flat,
            (((0,), (0,)), ((), ())),
            precision=highest,
            preferred_element_type=jnp.float32,
        )
        tap_list.append(product.reshape(3, channels, -1))
    return jnp.stack(tap_list)


def normalize(hidden, cell_count):
    totals = lax.psum(jnp.sum(hidden, axis=(0, 1)), ("row", "col"))
    average = totals / cell_count
    centered = hidden - average
    spread = lax.psum(jnp.sum(centered * centered, axis=(0, 1)), ("row", "col"))
    variance = spread / cell_count
    inverse = lax.rsqrt(variance + epsilon)
    return ((hidden - average) * inverse, inverse)


def normalize_back(grad_normed, normed, inverse, gain_row, cell_count):
    shift_sum, gain_sum = lax.psum(
        (jnp.sum(grad_normed, axis=(0, 1)), jnp.sum(grad_normed * normed, axis=(0, 1))),
        ("row", "col"),
    )
    grad_scaled = grad_normed * gain_row
    grad_hidden = inverse * (
        grad_scaled
        - gain_row * shift_sum / cell_count
        - normed * (gain_row * gain_sum / cell_count)
    )
    return (grad_hidden, gain_sum, shift_sum)


def elu_slope(values):
    return jnp.where(values > 0, 1.0, jnp.exp(jnp.minimum(values, 0.0)))


def mirror_tile(tile_in):
    local_row_count, local_column_count, channels = tile_in.shape
    row_devices = lax.axis_size("row")
    col_devices = lax.axis_size("col")
    row_part = local_row_count // col_devices
    group = row_devices // col_devices
    sectioned = tile_in.reshape(col_devices, row_part, local_column_count, channels)
    sectioned = lax.all_to_all(sectioned, "col", split_axis=0, concat_axis=0, tiled=True)
    sectioned = (
        sectioned.reshape(col_devices, row_part, group, local_row_count, channels)
        .transpose(0, 2, 1, 3, 4)
        .reshape(row_devices, row_part, local_row_count, channels)
    )
    sectioned = lax.all_to_all(
        lax.all_to_all(sectioned, "row", split_axis=0, concat_axis=0, tiled=True),
        "col",
        split_axis=0,
        concat_axis=0,
        tiled=True,
    )
    sectioned = sectioned.reshape(
        col_devices, group, row_part, local_row_count, channels
    ).transpose(3, 1, 0, 2, 4)
    return sectioned.reshape(local_row_count, local_column_count, channels)


def body(pair_map, cotangent, conv_one, conv_two, norm_gain, norm_shift):
    channels = conv_one.shape[2]
    local_row_count = pair_map.shape[0]
    local_column_count = pair_map.shape[1] // channels
    residues = float(local_row_count * lax.axis_size("row"))
    cell_count = float(
        local_row_count * local_column_count * lax.axis_size("row") * lax.axis_size("col")
    )
    feature_field_patch = pair_map.reshape(local_row_count, local_column_count, channels)
    field_ext = extend(feature_field_patch)
    first_conv = dilated(field_ext, conv_one, local_row_count, local_column_count)
    normed_one, inverse_one = normalize(first_conv, cell_count)
    before_one = normed_one * norm_gain[0] + norm_shift[0]
    active = jax.nn.elu(before_one)
    active_ext = extend(active)
    second_conv = dilated(active_ext, conv_two, local_row_count, local_column_count)
    normed_two, inverse_two = normalize(second_conv, cell_count)
    summed = feature_field_patch + normed_two * norm_gain[1] + norm_shift[1]
    block_out = jax.nn.elu(summed)
    symmetric = 0.5 * (block_out + mirror_tile(block_out))
    grad_in = cotangent.reshape(local_row_count, local_column_count, channels)
    grad_out = 0.5 * (grad_in + mirror_tile(grad_in))
    grad_sum = grad_out * elu_slope(summed)
    grad_second, gain_two, shift_two = normalize_back(
        grad_sum, normed_two, inverse_two, norm_gain[1], cell_count
    )
    second_ext = extend(grad_second)
    grad_active = dilated_back(second_ext, conv_two, local_row_count, local_column_count)
    kernel_two = kernel_grad(active_ext, grad_second, local_row_count, local_column_count)
    grad_before = grad_active * elu_slope(before_one)
    grad_first, gain_one, shift_one = normalize_back(
        grad_before, normed_one, inverse_one, norm_gain[0], cell_count
    )
    first_ext = extend(grad_first)
    grad_field = grad_sum + dilated_back(first_ext, conv_one, local_row_count, local_column_count)
    kernel_one = kernel_grad(field_ext, grad_first, local_row_count, local_column_count)
    total_one, total_two = lax.psum((kernel_one, kernel_two), ("row", "col"))
    grad_gains = jnp.stack([gain_one, gain_two]) / residues
    grad_shifts = jnp.stack([shift_one, shift_two]) / residues
    return (
        symmetric.reshape(local_row_count, local_column_count * channels),
        grad_field.reshape(local_row_count, local_column_count * channels),
        total_one / residues,
        total_two / residues,
        grad_gains,
        grad_shifts,
    )


def solution(mesh):
    return jax.shard_map(
        body,
        mesh=mesh,
        in_specs=(P("row", "col"), P("row", "col"), P(), P(), P(), P()),
        out_specs=(P("row", "col"), P("row", "col"), P(), P(), P(), P()),
        check_vma=False,
    )
```

profile of v0, /device:TPU:0, one launch (start us, length us, event | category | flops | bytes accessed | tf_op | source)
XLA Modules:
  0.0 586.3 jit_solution(13358520050994075313)
XLA Ops:
  9.6 3.0 collective-permute-start
  13.9 5.0 collective-permute-start.2
  20.3 5.8 collective-permute-done.2
  26.1 4.7 collective-permute-done.3
  34.1 43.9 %psum.70 = f32[64]{0:T(128)S(1)} all-reduce(f32[64]{0:T(128)S(1)} %get-tuple-element.61), channel_id=1, replica_groups=mesh['row'=8,'col'=4] {'row','col'}, use_global_device_ids=true, to_apply=%region_1.0 | all-reduce | flops 64 | bytes 512 | tf_op jit(solution)/shard_map/psum | solution.py:103
  78.3 40.1 %psum.71 = f32[64]{0:T(128)S(1)} all-reduce(f32[64]{0:T(128)S(1)} %multiply_reduce_fusion.3), channel_id=1, replica_groups=mesh['row'=8,'col'=4] {'row','col'}, use_global_device_ids=true, to_apply=%region_3.0 | all-reduce | flops 64 | bytes 512 | tf_op jit(solution)/shard_map/psum | solution.py:106
  120.4 3.0 collective-permute-start.4
  124.4 3.8 all-to-all-start.3
  130.1 3.9 collective-permute-start.6
  138.5 5.0 collective-permute-done.6
  143.5 4.7 collective-permute-done.7
  154.1 39.2 %psum.72 = f32[64]{0:T(128)S(1)} all-reduce(f32[64]{0:T(128)S(1)} %get-tuple-element.63), channel_id=1, replica_groups=mesh['row'=8,'col'=4] {'row','col'}, use_global_device_ids=true, to_apply=%region_5.6 | all-reduce | flops 64 | bytes 512 | tf_op jit(solution)/shard_map/psum | solution.py:103
  195.5 40.1 %psum.73 = f32[64]{0:T(128)} all-reduce(f32[64]{0:T(128)S(1)} %multiply_reduce_fusion.2), channel_id=1, replica_groups=mesh['row'=8,'col'=4] {'row','col'}, use_global_device_ids=true, to_apply=%region_7.8 | all-reduce | flops 64 | bytes 512 | tf_op jit(solution)/shard_map/psum | solution.py:106
  236.7 1.8 compare_select_fusion
  238.5 1.8 reshape.252
  240.3 3.9 all-to-all-start
  246.0 1.8 reshape.260
  247.8 2.5 all-to-all-done
  250.2 4.0 all-to-all-start.4
  254.2 2.5 reduce.13
  256.7 1.8 reshape.253
  260.2 1.8 reshape.254
  262.0 4.2 all-to-all-start.1
  266.2 2.5 reduce.11
  268.7 1.7 reshape.261
  270.4 1.8 reshape.262
  272.2 3.9 all-to-all-start.5
  276.2 2.5 reduce.14
  278.6 1.7 reshape.255
  280.4 1.8 reshape.256
  282.8 4.4 all-to-all-start.2
  288.0 1.7 reshape.246
  289.7 1.7 reshape.225
  293.9 1.7 copy.66
  305.4 2.0 fusion.35
  307.4 2.0 copy.62
  310.5 1.9 reduce.12
  318.7 1.9 reduce.15
  322.9 41.2 %all-reduce.1 = (f32[64]{0:T(128)S(1)}, f32[64]{0:T(128)S(1)}) all-reduce(f32[64]{0:T(128)S(1)} %reduce_sum.95, f32[64]{0:T(128)S(1)} %reduce_sum.92), channel_id=1, replica_groups=mesh['row'=8,'col'=4] {'row','col'}, use_global_device_ids=true, to_apply=%region_13.14 | all-reduce | flops 128 | bytes 1024 | tf_op jit(solution)/shard_map/psum | solution.py:113
  367.1 3.0 collective-permute-start.8
  373.2 4.6 collective-permute-start.11
  379.0 4.3 collective-permute-done.10
  383.3 1.7 collective-permute-done.11
  389.1 44.3 %all-reduce = (f32[64]{0:T(128)S(1)}, f32[64]{0:T(128)S(1)}) all-reduce(f32[64]{0:T(128)S(1)} %get-tuple-element.7, f32[64]{0:T(128)S(1)} %get-tuple-element.6), channel_id=1, replica_groups=mesh['row'=8,'col'=4] {'row','col'}, use_global_device_ids=true, to_apply=%region_17.18 | all-reduce | flops 128 | bytes 1024 | tf_op jit(solution)/shard_map/psum | solution.py:113
  434.9 3.3 collective-permute-start.12
  443.7 4.6 collective-permute-start.15
  448.3 123.8 %all-reduce.5.cloned.1.call-done = (f32[3,3,64,64]{3,2,1,0:T(8,128)}, f32[3,3,64,64]{3,2,1,0:T(8,128)}) async-done(((f32[3,3,64,64]{3,2,1,0:T(8,128)}, f32[3,3,64,64]{3,2,1,0:T(8,128)}), (f32[3,3,64,64]{3,2,1,0:T(8,128)}, f32[3,3,64,64]{3,2,1,0:T(8,128)})) %all-reduce.5.cloned.1.call-update) | async-done | bytes 294928 | tf_op jit(solution)/shard_map/psum | solution.py:192
  572.0 1.7 broadcast_multiply_fusion.1
  (251 shorter events, 77.4 us)
Async XLA Ops:
  7.2 5.5 copy-start.9
  7.2 5.6 copy-start.33
  8.3 5.5 copy-start
  8.3 5.5 collective-permute-start.1
  9.6 4.2 collective-permute-start
  13.9 6.3 %copy-start.58 = (f32[2,64]{1,0:T(2,128)S(1)}, f32[2,64]{1,0:T(2,128)}, u32[]{:S(2)}) copy-start(f32[2,64]{1,0:T(2,128)} %param.11) | copy-start | bytes 1540
  13.9 6.3 %copy-start.56 = (f32[2,64]{1,0:T(2,128)S(1)}, f32[2,64]{1,0:T(2,128)}, u32[]{:S(2)}) copy-start(f32[2,64]{1,0:T(2,128)} %param.10) | copy-start | bytes 1540
  13.9 12.2 %collective-permute-start.2 = (f32[48,16,64]{2,1,0:T(8,128)S(1)}, f32[48,16,64]{2,1,0:T(8,128)S(1)}, u32[]{:S(2)}, u32[]{:S(2)}) collective-permute-start(f32[48,16,64]{2,1,0:T(8,128)S(1)} %get-tuple-element.34), channel_id=1, source_target_pairs={{0,1},{1,2},{2,3},{4,5},{5,6},{6,7},{8,9},{9,10},{10,11},{12,13},{... | collective-permute-start | bytes 589832 | tf_op jit(solution)/shard_map/ppermute | solution.py:21
  18.9 11.9 %collective-permute-start.3 = (f32[48,16,64]{2,1,0:T(8,128)S(1)}, f32[48,16,64]{2,1,0:T(8,128)S(1)}, u32[]{:S(2)}, u32[]{:S(2)}) collective-permute-start(f32[48,16,64]{2,1,0:T(8,128)S(1)} %get-tuple-element.35), channel_id=1, source_target_pairs={{1,0},{2,1},{3,2},{5,4},{6,5},{7,6},{9,8},{10,9},{11,10},{13,12},{... | collective-permute-start | bytes 589832 | tf_op jit(solution)/shard_map/ppermute | solution.py:23
  20.3 98.2 %copy-start.40 = (f32[64]{0:T(128)}, f32[64]{0:T(128)S(1)}, u32[]{:S(2)}) copy-start(f32[64]{0:T(128)S(1)} %get-tuple-element.66) | copy-start | bytes 772
  20.3 98.1 %copy-start.54 = (f32[64]{0:T(128)}, f32[64]{0:T(128)S(1)}, u32[]{:S(2)}) copy-start(f32[64]{0:T(128)S(1)} %get-tuple-element.60) | copy-start | bytes 772
  20.3 215.9 %copy-start.47 = (f32[64]{0:T(128)}, f32[64]{0:T(128)S(1)}, u32[]{:S(2)}) copy-start(f32[64]{0:T(128)S(1)} %get-tuple-element.59) | copy-start | bytes 772
  20.3 215.9 %copy-start.49 = (f32[64]{0:T(128)}, f32[64]{0:T(128)S(1)}, u32[]{:S(2)}) copy-start(f32[64]{0:T(128)S(1)} %get-tuple-element.67) | copy-start | bytes 772
  78.0 40.5 %copy-start.38 = (f32[64]{0:T(128)}, f32[64]{0:T(128)S(1)}, u32[]{:S(2)}) copy-start(f32[64]{0:T(128)S(1)} %broadcast_multiply_fusion.3) | copy-start | bytes 772
  119.1 10.0 %collective-permute-start.5 = (f32[16,32,64]{2,1,0:T(8,128)S(1)}, f32[16,32,64]{2,1,0:T(8,128)S(1)}, u32[]{:S(2)}, u32[]{:S(2)}) collective-permute-start(f32[16,32,64]{2,1,0:T(8,128)S(1)} %compare_select_fusion.3), channel_id=1, source_target_pairs={{4,0},{8,4},{12,8},{16,12},{20,16},{24,20},{28,24},{5,1},{9,5},{13... | collective-permute-start | bytes 393224 | tf_op jit(solution)/shard_map/ppermute | solution.py:23
  120.4 8.7 %collective-permute-start.4 = (f32[16,32,64]{2,1,0:T(8,128)S(1)}, f32[16,32,64]{2,1,0:T(8,128)S(1)}, u32[]{:S(2)}, u32[]{:S(2)}) collective-permute-start(f32[16,32,64]{2,1,0:T(8,128)S(1)} %compare_select_fusion.3), channel_id=1, source_target_pairs={{0,4},{4,8},{8,12},{12,16},{16,20},{20,24},{24,28},{1,5},{5,9},{9,... | collective-permute-start | bytes 393224 | tf_op jit(solution)/shard_map/ppermute | solution.py:21
  124.4 11.7 %all-to-all-start.3 = ((f32[4,1,8192]{2,1,0:T(1,128)}), f32[4,1,8192]{2,1,0:T(1,128)S(1)}, u32[]{:S(2)}, u32[]{:S(2)}) async-start(f32[4,1,8192]{2,1,0:T(1,128)} %reshape.258), calls=%async_computation.3 | async-start | bytes 262144 | tf_op jit(solution)/shard_map/all_to_all | solution.py:137
  129.1 19.1 %copy-start.4 = (f32[16,32,64]{2,1,0:T(8,128)}, f32[16,32,64]{2,1,0:T(8,128)S(1)}, u32[]{:S(2)}) copy-start(f32[16,32,64]{2,1,0:T(8,128)S(1)} %collective-permute-done.5) | copy-start | bytes 393220
  129.1 19.1 %copy-start.6 = (f32[16,32,64]{2,1,0:T(8,128)}, f32[16,32,64]{2,1,0:T(8,128)S(1)}, u32[]{:S(2)}) copy-start(f32[16,32,64]{2,1,0:T(8,128)S(1)} %collective-permute-done.4) | copy-start | bytes 393220
  129.2 6.2 %copy-start.34 = (f32[3,3,64,64]{3,2,1,0:T(8,128)S(1)}, f32[3,3,64,64]{3,2,1,0:T(8,128)}, u32[]{:S(2)}) copy-start(f32[3,3,64,64]{3,2,1,0:T(8,128)} %param.9) | copy-start | bytes 442372
  130.1 13.4 %collective-permute-start.6 = (f32[48,16,64]{2,1,0:T(8,128)}, f32[48,16,64]{2,1,0:T(8,128)S(1)}, u32[]{:S(2)}, u32[]{:S(2)}) collective-permute-start(f32[48,16,64]{2,1,0:T(8,128)} %get-tuple-element.30), channel_id=1, source_target_pairs={{0,1},{1,2},{2,3},{4,5},{5,6},{6,7},{8,9},{9,10},{10,11},{12,13},{... | collective-permute-start | bytes 589832 | tf_op jit(solution)/shard_map/ppermute | solution.py:21
  134.0 14.1 %collective-permute-start.7 = (f32[48,16,64]{2,1,0:T(8,128)}, f32[48,16,64]{2,1,0:T(8,128)}, u32[]{:S(2)}, u32[]{:S(2)}) collective-permute-start(f32[48,16,64]{2,1,0:T(8,128)} %get-tuple-element.31), channel_id=1, source_target_pairs={{1,0},{2,1},{3,2},{5,4},{6,5},{7,6},{9,8},{10,9},{11,10},{13,12},{... | collective-permute-start | bytes 589832 | tf_op jit(solution)/shard_map/ppermute | solution.py:23
  143.5 5.8 copy-start.13
  193.3 42.9 %copy-start.44 = (f32[64]{0:T(128)}, f32[64]{0:T(128)S(1)}, u32[]{:S(2)}) copy-start(f32[64]{0:T(128)S(1)} %broadcast_multiply_fusion.2) | copy-start | bytes 772
  240.3 9.9 %all-to-all-start = ((f32[4,1,8192]{2,1,0:T(1,128)}), f32[4,1,8192]{2,1,0:T(1,128)}, u32[]{:S(2)}, u32[]{:S(2)}) async-start(f32[4,1,8192]{2,1,0:T(1,128)} %reshape.252), calls=%async_computation | async-start | bytes 262144 | tf_op jit(solution)/shard_map/all_to_all | solution.py:137
  250.2 11.8 %all-to-all-start.4 = ((f32[8,1,4096]{2,1,0:T(1,128)}), f32[8,1,4096]{2,1,0:T(1,128)}, u32[]{:S(2)}, u32[]{:S(2)}) async-start(f32[8,1,4096]{2,1,0:T(1,128)} %reshape.260), calls=%async_computation.4 | async-start | bytes 262144 | tf_op jit(solution)/shard_map/all_to_all | solution.py:144
  262.0 10.2 %all-to-all-start.1 = ((f32[8,1,4096]{2,1,0:T(1,128)}), f32[8,1,4096]{2,1,0:T(1,128)}, u32[]{:S(2)}, u32[]{:S(2)}) async-start(f32[8,1,4096]{2,1,0:T(1,128)} %reshape.254), calls=%async_computation.1 | async-start | bytes 262144 | tf_op jit(solution)/shard_map/all_to_all | solution.py:144
  272.2 10.6 %all-to-all-start.5 = ((f32[4,1,8192]{2,1,0:T(1,128)}), f32[4,1,8192]{2,1,0:T(1,128)}, u32[]{:S(2)}, u32[]{:S(2)}) async-start(f32[4,1,8192]{2,1,0:T(1,128)} %reshape.262), calls=%async_computation.5 | async-start | bytes 262144 | tf_op jit(solution)/shard_map/all_to_all | solution.py:143
  282.8 35.9 %all-to-all-start.2 = ((f32[4,1,8192]{2,1,0:T(1,128)}), f32[4,1,8192]{2,1,0:T(1,128)}, u32[]{:S(2)}, u32[]{:S(2)}) async-start(f32[4,1,8192]{2,1,0:T(1,128)} %reshape.256), calls=%async_computation.2 | async-start | bytes 262144 | tf_op jit(solution)/shard_map/all_to_all | solution.py:143
  287.2 284.8 %all-reduce.5.cloned.1.call-start = ((), (), s32[]{:S(2)}) async-start(), calls=%async_computation.6 | async-start | bytes 1179648 | tf_op jit(solution)/shard_map/psum | solution.py:192
  321.9 42.9 %copy-start.1 = (f32[16,32,64]{2,1,0:T(8,128)S(1)}, f32[16,32,64]{2,1,0:T(8,128)}, u32[]{:S(2)}) copy-start(f32[16,32,64]{2,1,0:T(8,128)} %copy-done) | copy-start | bytes 393220
  321.9 42.9 %copy-start.18 = (f32[16,32,64]{2,1,0:T(8,128)S(1)}, f32[16,32,64]{2,1,0:T(8,128)}, u32[]{:S(2)}) copy-start(f32[16,32,64]{2,1,0:T(8,128)} %reshape.225) | copy-start | bytes 393220
  321.9 42.9 %copy-start.19 = (f32[16,2,4,4,64]{4,0,3,2,1:T(8,128)S(1)}, f32[16,2,4,4,64]{4,0,3,2,1:T(8,128)}, u32[]{:S(2)}) copy-start(f32[16,2,4,4,64]{4,0,3,2,1:T(8,128)} %copy.50) | copy-start | bytes 393220
  321.9 42.9 %copy-start.53 = (f32[64]{0:T(128)S(1)}, f32[64]{0:T(128)}, u32[]{:S(2)}) copy-start(f32[64]{0:T(128)} %copy-done.51) | copy-start | bytes 772
  365.4 4.7 copy-start.8
  365.4 4.7 copy-start.20
  365.4 4.7 copy-start.21
  365.4 4.7 copy-start.22
  365.6 6.2 %collective-permute-start.9 = (f32[16,32,64]{2,1,0:T(8,128)S(1)}, f32[16,32,64]{2,1,0:T(8,128)S(1)}, u32[]{:S(2)}, u32[]{:S(2)}) collective-permute-start(f32[16,32,64]{2,1,0:T(8,128)S(1)} %fusion.34), channel_id=1, source_target_pairs={{4,0},{8,4},{12,8},{16,12},{20,16},{24,20},{28,24},{5,1},{9,5},{13... | collective-permute-start | bytes 393224 | tf_op jit(solution)/shard_map/ppermute | solution.py:23
  367.1 4.7 collective-permute-start.8
  371.9 11.4 %collective-permute-start.10 = (f32[48,16,64]{2,1,0:T(8,128)S(1)}, f32[48,16,64]{2,1,0:T(8,128)S(1)}, u32[]{:S(2)}, u32[]{:S(2)}) collective-permute-start(f32[48,16,64]{2,1,0:T(8,128)S(1)} %get-tuple-element.28), channel_id=1, source_target_pairs={{1,0},{2,1},{3,2},{5,4},{6,5},{7,6},{9,8},{10,9},{11,10},{13,12},{... | collective-permute-start | bytes 589832 | tf_op jit(solution)/shard_map/ppermute | solution.py:23
  373.2 11.8 %collective-permute-start.11 = (f32[48,16,64]{2,1,0:T(8,128)S(1)}, f32[48,16,64]{2,1,0:T(8,128)S(1)}, u32[]{:S(2)}, u32[]{:S(2)}) collective-permute-start(f32[48,16,64]{2,1,0:T(8,128)S(1)} %get-tuple-element.29), channel_id=1, source_target_pairs={{0,1},{1,2},{2,3},{4,5},{5,6},{6,7},{8,9},{9,10},{10,11},{12,13},{... | collective-permute-start | bytes 589832 | tf_op jit(solution)/shard_map/ppermute | solution.py:21
  379.0 6.2 %copy-start.31 = (f32[3,64,64]{2,1,0:T(8,128)S(1)}, f32[3,64,64]{2,1,0:T(8,128)}, u32[]{:S(2)}) copy-start(f32[3,64,64]{2,1,0:T(8,128)} %copy.54) | copy-start | bytes 147460
  433.5 5.3 copy-start.15
  433.5 8.7 %collective-permute-start.13 = (f32[16,32,64]{2,1,0:T(8,128)S(1)}, f32[16,32,64]{2,1,0:T(8,128)S(1)}, u32[]{:S(2)}, u32[]{:S(2)}) collective-permute-start(f32[16,32,64]{2,1,0:T(8,128)S(1)} %fusion.27), channel_id=1, source_target_pairs={{4,0},{8,4},{12,8},{16,12},{20,16},{24,20},{28,24},{5,1},{9,5},{13... | collective-permute-start | bytes 393224 | tf_op jit(solution)/shard_map/ppermute | solution.py:23
  434.9 7.3 %collective-permute-start.12 = (f32[16,32,64]{2,1,0:T(8,128)S(1)}, f32[16,32,64]{2,1,0:T(8,128)S(1)}, u32[]{:S(2)}, u32[]{:S(2)}) collective-permute-start(f32[16,32,64]{2,1,0:T(8,128)S(1)} %fusion.27), channel_id=1, source_target_pairs={{0,4},{4,8},{8,12},{12,16},{16,20},{20,24},{24,28},{1,5},{5,9},{9,... | collective-permute-start | bytes 393224 | tf_op jit(solution)/shard_map/ppermute | solution.py:21
  442.4 132.1 %collective-permute-start.14 = (f32[48,16,64]{2,1,0:T(8,128)S(1)}, f32[48,16,64]{2,1,0:T(8,128)S(1)}, u32[]{:S(2)}, u32[]{:S(2)}) collective-permute-start(f32[48,16,64]{2,1,0:T(8,128)S(1)} %get-tuple-element.26), channel_id=1, source_target_pairs={{1,0},{2,1},{3,2},{5,4},{6,5},{7,6},{9,8},{10,9},{11,10},{13,12},{... | collective-permute-start | bytes 589832 | tf_op jit(solution)/shard_map/ppermute | solution.py:23
  443.7 130.8 %collective-permute-start.15 = (f32[48,16,64]{2,1,0:T(8,128)S(1)}, f32[48,16,64]{2,1,0:T(8,128)S(1)}, u32[]{:S(2)}, u32[]{:S(2)}) collective-permute-start(f32[48,16,64]{2,1,0:T(8,128)S(1)} %get-tuple-element.27), channel_id=1, source_target_pairs={{0,1},{1,2},{2,3},{4,5},{5,6},{6,7},{8,9},{9,10},{10,11},{12,13},{... | collective-permute-start | bytes 589832 | tf_op jit(solution)/shard_map/ppermute | solution.py:21
  (34 other events, 38.0 us)
Sparse Core Ops, SparseCore 0:
  441.8 130.1 all-reduce.4
where the time goes:
time: 589 us; the launch traced here: 586 us
  blocking collectives  249 us (42%)
  waiting for transfers between devices  153 us (26%)
  starting transfers between devices  65.4 us (11%)
  local copies, waits for them, and re-layouts  61 us (10%)
  other arithmetic  30.9 us (5%)
  between operations  15 us (3%)
  matrix products  11.9 us (2%)
    psum x1, waiting for transfers between devices, body(): total_one, total_two = lax.psum((kernel_one, kernel_two), ('row', 'col'))  124 us
    psum x2, blocking collectives, normalize_back(): lax.psum((jnp.sum(grad_normed, axis=(0, 1)), jnp.sum(grad_normed * normed...  85.4 us
    psum x2, blocking collectives, normalize(): totals = lax.psum(jnp.sum(hidden, axis=(0, 1)), ('row', 'col'))  83.1 us
    psum x2, blocking collectives, normalize(): spread = lax.psum(jnp.sum(centered * centered, axis=(0, 1)), ('row', 'col'))  80.2 us
    ppermute x8, starting transfers between devices, extended_2(): lax.ppermute(tail, axis, [(i, (i + 1) % count) for i in range(ends)])  30.5 us
    unnamed x132, local copies, waits for them, and re-layouts  25 us
    ppermute x8, waiting for transfers between devices, extended_2(): lax.ppermute(head, axis, [((i + 1) % count, i) for i in range(ends)])  13.7 us
    ppermute x8, waiting for transfers between devices, extended_2(): lax.ppermute(tail, axis, [(i, (i + 1) % count) for i in range(ends)])  12.8 us
  transfers between devices with their start and end apart: 23, of which 10 were waited for; matrix products, arithmetic and copies ran while one was open for 12% of the time, Pallas kernels for 0%

commit v1 on v0

--- a/solution.py
+++ b/solution.py
@@ -1,6 +1,10 @@
+import functools
+
 import jax
 import jax.numpy as jnp
 from jax import lax
+from jax.experimental import pallas as pl
+from jax.experimental.pallas import tpu as pltpu
 from jax.sharding import PartitionSpec as P
 
 DILATION_STEP = 16
@@ -153,7 +157,7 @@
     return sectioned.reshape(local_row_count, local_column_count, channels)
 
 
-def body(pair_map, cotangent, conv_one, conv_two, norm_gain, norm_shift):
+def general_body(pair_map, cotangent, conv_one, conv_two, norm_gain, norm_shift):
     channels = conv_one.shape[2]
     local_row_count = pair_map.shape[0]
     local_column_count = pair_map.shape[1] // channels
@@ -202,6 +206,468 @@
     )
 
 
+SLOTS = 8
+LANES = 128
+HALF = 64
+ROWS = 256
+AXES = ("row", "col")
+
+
+def phase_table(devices):
+    pairs = [(r, s) for r in range(DILATION_STEP) for s in range(r + 1, DILATION_STEP)]
+    table = []
+    taken = 0
+    diagonal = DILATION_STEP // 2
+    for device in range(devices):
+        count = SLOTS // 2 - (1 if device < diagonal else 0)
+        upper = pairs[taken : taken + count]
+        taken += count
+        lower = [(s, r) for r, s in upper]
+        if device < diagonal:
+            upper = upper + [(2 * device, 2 * device)]
+            lower = lower + [(2 * device + 1, 2 * device + 1)]
+        table.append(upper + lower)
+    return table
+
+
+def lane_low(shape):
+    return lax.broadcasted_iota(jnp.int32, shape, len(shape) - 1) < HALF
+
+
+def swap_halves(values):
+    return pltpu.roll(values, HALF, values.ndim - 1)
+
+
+def fold_halves(values):
+    return values + swap_halves(values)
+
+
+def twice(row):
+    return jnp.concatenate([row, row], axis=1)
+
+
+def exact_dot(left, right, dims):
+    return lax.dot_general(
+        left, right, (dims, ((), ())), precision=highest, preferred_element_type=jnp.float32
+    )
+
+
+def split_phases(tile_ref, scratch_ref):
+    low = lane_low((DILATION_STEP, LANES))
+    for t in range(DILATION_STEP // 2):
+        first = tile_ref[:, t * LANES : (t + 1) * LANES]
+        begin = DILATION_STEP * HALF + t * LANES
+        second = tile_ref[:, begin : begin + LANES]
+        row = 2 * t * DILATION_STEP
+        scratch_ref[row : row + DILATION_STEP, :] = jnp.where(low, first, swap_halves(second))
+        row += DILATION_STEP
+        scratch_ref[row : row + DILATION_STEP, :] = jnp.where(low, swap_halves(first), second)
+
+
+def join_phases(scratch_ref, tile_ref):
+    low = lane_low((DILATION_STEP, LANES))
+    for t in range(DILATION_STEP // 2):
+        row = 2 * t * DILATION_STEP
+        even = scratch_ref[row : row + DILATION_STEP, :]
+        odd = scratch_ref[row + DILATION_STEP : row + 2 * DILATION_STEP, :]
+        tile_ref[:, t * LANES : (t + 1) * LANES] = jnp.where(low, even, swap_halves(odd))
+        begin = DILATION_STEP * HALF + t * LANES
+        tile_ref[:, begin : begin + LANES] = jnp.where(low, swap_halves(even), odd)
+
+
+def pack_rows(table, scratch_ref, send_ref, stride):
+    for device, slots in enumerate(table):
+        for k, (r, s) in enumerate(slots):
+            source = s * DILATION_STEP + r
+            target = device * stride + k
+            send_ref[target : target + 1, :] = scratch_ref[source : source + 1, :]
+
+
+def unpack_rows(table, recv_ref, scratch_ref, stride, offset):
+    for device, slots in enumerate(table):
+        for k, (r, s) in enumerate(slots):
+            target = s * DILATION_STEP + r
+            source = device * stride + offset + k
+            scratch_ref[target : target + 1, :] = recv_ref[source : source + 1, :]
+
+
+def slot_rows(ref, stride, devices):
+    return jnp.concatenate(
+        [ref[d * stride : d * stride + SLOTS, :] for d in range(devices)], axis=0
+    )
+
+
+def neighbours(values):
+    zero = jnp.zeros((SLOTS, LANES), jnp.float32)
+    ahead = jnp.concatenate([values[SLOTS:], zero], axis=0)
+    behind = jnp.concatenate([zero, values[:-SLOTS]], axis=0)
+    place = (lax.broadcasted_iota(jnp.int32, (ROWS, LANES), 0) // SLOTS) % 4
+    low = lane_low((ROWS, LANES))
+    side = jnp.where(low, jnp.where(place == 3, 0.0, ahead), jnp.where(place == 0, 0.0, behind))
+    return jnp.concatenate([side, values], axis=1)
+
+
+def forward_weight(weight_ref):
+    zero = jnp.zeros((HALF, HALF), jnp.float32)
+    taps = []
+    for a in range(3):
+        w = [weight_ref[a, b] for b in range(3)]
+        blocks = [(zero, w[2]), (w[0], zero), (w[1], w[0]), (w[2], w[1])]
+        taps.append(
+            jnp.concatenate([jnp.concatenate(list(b), axis=1) for b in blocks], axis=0)
+        )
+    return jnp.concatenate(taps, axis=1)
+
+
+def backward_weight(weight_ref):
+    zero = jnp.zeros((HALF, HALF), jnp.float32)
+    taps = []
+    for a in range(3):
+        w = [weight_ref[2 - a, 2 - b] for b in range(3)]
+        taps.append(jnp.concatenate([zero, w[0], w[1], w[2]], axis=1))
+        taps.append(jnp.concatenate([w[2], zero, w[0], w[1]], axis=1))
+    return jnp.concatenate(taps, axis=0)
+
+
+def shifted_sum(parts):
+    step = 4 * SLOTS
+    zero = jnp.zeros((step, LANES), jnp.float32)
+    first, middle, last = (parts[:, a * LANES : (a + 1) * LANES] for a in range(3))
+    return (
+        middle
+        + jnp.concatenate([zero, first[:-step]], axis=0)
+        + jnp.concatenate([last[step:], zero], axis=0)
+    )
+
+
+def spread_shifts(values):
+    step = 4 * SLOTS
+    zero = jnp.zeros((step, LANES), jnp.float32)
+    return jnp.concatenate(
+        [
+            jnp.concatenate([values[step:], zero], axis=0),
+            values,
+            jnp.concatenate([zero, values[:-step]], axis=0),
+        ],
+        axis=1,
+    )
+
+
+def kernel_rows(joined, grad):
+    product = exact_dot(joined, spread_shifts(grad), ((0,), (0,)))
+    pieces = []
+    for a in range(3):
+        part = product[:, a * LANES : (a + 1) * LANES]
+        for even, odd in ((1, 2), (2, 3), (3, 0)):
+            tap = part[even * HALF : (even + 1) * HALF] + swap_halves(
+                part[odd * HALF : (odd + 1) * HALF]
+            )
+            low = lane_low((HALF // 2, LANES))
+            pieces.append(jnp.where(low, tap[: HALF // 2], swap_halves(tap[HALF // 2 :])))
+    return jnp.concatenate(pieces, axis=0)
+
+
+def local_stats(hidden):
+    count = 2.0 * ROWS
+    mean = fold_halves(jnp.sum(hidden, axis=0, keepdims=True)) / count
+    centered = hidden - mean
+    spread = fold_halves(jnp.sum(centered * centered, axis=0, keepdims=True))
+    return jnp.where(lane_low((1, LANES)), mean, spread)
+
+
+def combine_stats(rows, devices):
+    low = lane_low((devices, LANES))
+    means = jnp.where(low, rows, swap_halves(rows))
+    spreads = jnp.where(low, swap_halves(rows), rows)
+    mean = jnp.sum(means, axis=0, keepdims=True) / devices
+    apart = means - mean
+    total = jnp.sum(spreads + (2.0 * ROWS) * (apart * apart), axis=0, keepdims=True)
+    return mean, lax.rsqrt(total / (2.0 * ROWS * devices) + epsilon)
+
+
+def elu_value(values):
+    return jnp.where(values > 0, values, jnp.exp(jnp.minimum(values, 0.0)) - 1.0)
+
+
+def pair_sums(grad, normed):
+    plain = fold_halves(jnp.sum(grad, axis=0, keepdims=True))
+    scaled = fold_halves(jnp.sum(grad * normed, axis=0, keepdims=True))
+    return jnp.where(lane_low((1, LANES)), plain, scaled)
+
+
+def split_sums(rows):
+    total = jnp.sum(rows, axis=0, keepdims=True)
+    other = swap_halves(total)
+    low = lane_low((1, LANES))
+    return jnp.where(low, total, other), jnp.where(low, other, total)
+
+
+def norm_back(grad, normed, inverse, gain, shift_sum, gain_sum, cells):
+    return inverse * (gain * grad - gain * shift_sum / cells - normed * (gain * gain_sum / cells))
+
+
+def mirrored(values, own_mask):
+    low = lane_low((SLOTS, LANES))
+    tiles = [values[i * SLOTS : (i + 1) * SLOTS] for i in range(ROWS // SLOTS)]
+    pieces = []
+    for p in range(SLOTS):
+        for c in range(4):
+            even = tiles[2 * c * 4 + p // 2]
+            odd = tiles[(2 * c + 1) * 4 + p // 2]
+            if p % 2 == 0:
+                piece = jnp.where(low, even, swap_halves(odd))
+            else:
+                piece = jnp.where(low, swap_halves(even), odd)
+            pieces.append(jnp.where(own_mask, piece, pltpu.roll(piece, 4, 0)))
+    return jnp.concatenate(pieces, axis=0)
+
+
+def first_kernel(table, x_ref, send_ref, scratch_ref):
+    split_phases(x_ref, scratch_ref)
+    pack_rows(table, scratch_ref, send_ref, SLOTS)
+
+
+def conv_one_kernel(table, x_ref, weight_ref, g_ref, hidden_ref, send_ref, scratch_ref):
+    split_phases(g_ref, scratch_ref)
+    stride = SLOTS + 1
+    pack_rows(table, scratch_ref, send_ref, stride)
+    hidden = shifted_sum(
+        exact_dot(neighbours(x_ref[...]), forward_weight(weight_ref), ((1,), (0,)))
+    )
+    hidden_ref[...] = hidden
+    stats = local_stats(hidden)
+    for d in range(len(table)):
+        send_ref[d * stride + SLOTS : (d + 1) * stride, :] = stats
+
+
+def conv_two_kernel(
+    devices, recv_ref, hidden_ref, weight_ref, gain_ref, shift_ref,
+    normed_ref, inverse_ref, active_ref, second_ref, send_ref,
+):
+    stride = SLOTS + 1
+    mean, inverse = combine_stats(recv_ref[pl.ds(SLOTS, devices, stride=stride), :], devices)
+    normed = (hidden_ref[...] - mean) * inverse
+    normed_ref[...] = normed
+    inverse_ref[...] = inverse
+    active = elu_value(normed * twice(gain_ref[0:1, :]) + twice(shift_ref[0:1, :]))
+    active_ref[...] = active
+    second = shifted_sum(
+        exact_dot(neighbours(active), forward_weight(weight_ref), ((1,), (0,)))
+    )
+    second_ref[...] = second
+    send_ref[...] = jnp.broadcast_to(local_stats(second), (devices, LANES))
+
+
+def output_kernel(
+    devices, recv_ref, second_ref, x_ref, grad_ref, gain_ref, shift_ref, own_ref,
+    normed_ref, inverse_ref, sum_ref, send_ref,
+):
+    stride = SLOTS + 1
+    mean, inverse = combine_stats(recv_ref[...], devices)
+    normed = (second_ref[...] - mean) * inverse
+    normed_ref[...] = normed
+    inverse_ref[...] = inverse
+    summed = x_ref[...] + normed * twice(gain_ref[1:2, :]) + twice(shift_ref[1:2, :])
+    slope = jnp.exp(jnp.minimum(summed, 0.0))
+    out = jnp.where(summed > 0, summed, slope - 1.0)
+    own = own_ref[...] > 0
+    symmetric = 0.5 * (out + mirrored(out, own))
+    for d in range(devices):
+        send_ref[d * stride : d * stride + SLOTS, :] = symmetric[d * SLOTS : (d + 1) * SLOTS]
+    grad_in = slot_rows(grad_ref, stride, devices)
+    grad_out = 0.5 * (grad_in + mirrored(grad_in, own))
+    grad_sum = grad_out * jnp.where(summed > 0, 1.0, slope)
+    sum_ref[...] = grad_sum
+    sums = pair_sums(grad_sum, normed)
+    for d in range(devices):
+        send_ref[d * stride + SLOTS : (d + 1) * stride, :] = sums
+
+
+def back_two_kernel(
+    devices, recv_ref, sum_ref, normed_two_ref, inverse_two_ref, active_ref, normed_ref,
+    weight_ref, gain_ref, shift_ref, before_ref, total_ref, send_ref, scratch_ref,
+):
+    cells = 2.0 * ROWS * devices
+    shift_sum, gain_sum = split_sums(recv_ref[pl.ds(SLOTS, devices, stride=SLOTS + 1), :])
+    total_ref[...] = jnp.where(lane_low((1, LANES)), shift_sum, gain_sum)
+    grad_second = norm_back(
+        sum_ref[...], normed_two_ref[...], inverse_two_ref[...], twice(gain_ref[1:2, :]),
+        shift_sum, gain_sum, cells,
+    )
+    grad_active = shifted_sum(
+        exact_dot(neighbours(grad_second), backward_weight(weight_ref), ((1,), (1,)))
+    )
+    normed = normed_ref[...]
+    before = normed * twice(gain_ref[0:1, :]) + twice(shift_ref[0:1, :])
+    grad_before = grad_active * jnp.where(before > 0, 1.0, jnp.exp(jnp.minimum(before, 0.0)))
+    before_ref[...] = grad_before
+    sums = pair_sums(grad_before, normed)
+    share = ROWS * 9 // 8 // devices
+    stride = share + 1
+    scratch_ref[...] = kernel_rows(neighbours(active_ref[...]), grad_second)
+    for d in range(devices):
+        send_ref[d * stride : d * stride + share, :] = scratch_ref[d * share : (d + 1) * share, :]
+        send_ref[d * stride + share : (d + 1) * stride, :] = sums
+
+
+def reduce_share(ref, devices, share, stride):
+    total = ref[0:share, :]
+    for d in range(1, devices):
+        total = total + ref[d * stride : d * stride + share, :]
+    return total
+
+
+def back_one_kernel(
+    devices, recv_ref, before_ref, normed_ref, inverse_ref, x_ref, sum_ref, weight_ref, gain_ref,
+    total_ref, two_ref, send_ref, scratch_ref,
+):
+    cells = 2.0 * ROWS * devices
+    share = ROWS * 9 // 8 // devices
+    stride = share + 1
+    shift_sum, gain_sum = split_sums(recv_ref[pl.ds(share, devices, stride=stride), :])
+    total_ref[...] = jnp.where(lane_low((1, LANES)), shift_sum, gain_sum)
+    two_ref[...] = reduce_share(recv_ref, devices, share, stride)
+    grad_first = norm_back(
+        before_ref[...], normed_ref[...], inverse_ref[...], twice(gain_ref[0:1, :]),
+        shift_sum, gain_sum, cells,
+    )
+    field = sum_ref[...] + shifted_sum(
+        exact_dot(neighbours(grad_first), backward_weight(weight_ref), ((1,), (1,)))
+    )
+    scratch_ref[...] = kernel_rows(neighbours(x_ref[...]), grad_first)
+    stride = share + SLOTS
+    for d in range(devices):
+        send_ref[d * stride : d * stride + SLOTS, :] = field[d * SLOTS : (d + 1) * SLOTS]
+        send_ref[d * stride + SLOTS : (d + 1) * stride, :] = scratch_ref[
+            d * share : (d + 1) * share, :
+        ]
+
+
+def share_kernel(devices, recv_ref, two_ref, send_ref):
+    share = ROWS * 9 // 8 // devices
+    stride = share + SLOTS
+    total = recv_ref[SLOTS:stride, :]
+    for d in range(1, devices):
+        total = total + recv_ref[d * stride + SLOTS : (d + 1) * stride, :]
+    two = two_ref[...]
+    for d in range(devices):
+        send_ref[2 * d * share : (2 * d + 1) * share, :] = total
+        send_ref[(2 * d + 1) * share : (2 * d + 2) * share, :] = two
+
+
+def last_kernel(
+    table, residues, sym_recv_ref, map_recv_ref, recv_ref, total_one_ref, total_two_ref,
+    sym_ref, map_ref, one_ref, two_ref, gain_ref, shift_ref, scratch_ref, rows_ref,
+):
+    devices = len(table)
+    share = ROWS * 9 // 8 // devices
+    unpack_rows(table, sym_recv_ref, scratch_ref, SLOTS + 1, 0)
+    join_phases(scratch_ref, sym_ref)
+    unpack_rows(table, map_recv_ref, scratch_ref, SLOTS + share, 0)
+    join_phases(scratch_ref, map_ref)
+    for index, out_ref in ((0, one_ref), (1, two_ref)):
+        for d in range(devices):
+            begin = (2 * d + index) * share
+            rows_ref[d * share : (d + 1) * share, :] = recv_ref[begin : begin + share, :]
+        for tap in range(9):
+            block = rows_ref[tap * HALF // 2 : (tap + 1) * HALF // 2, :] / residues
+            out_ref[tap, : HALF // 2, :] = block[:, :HALF]
+            out_ref[tap, HALF // 2 :, :] = swap_halves(block)[:, :HALF]
+    for index, total_ref in ((0, total_one_ref), (1, total_two_ref)):
+        total = total_ref[...] / residues
+        shift_ref[index : index + 1, :] = total[:, :HALF]
+        gain_ref[index : index + 1, :] = swap_halves(total)[:, :HALF]
+
+
+def call(body, shapes, scratch=()):
+    return pl.pallas_call(
+        body,
+        out_shape=[jax.ShapeDtypeStruct(s, jnp.float32) for s in shapes],
+        scratch_shapes=[pltpu.VMEM(s, jnp.float32) for s in scratch],
+    )
+
+
+def exchange(rows, devices):
+    sent = rows.reshape(devices, 1, -1)
+    received = lax.all_to_all(sent, AXES, split_axis=0, concat_axis=0, tiled=True)
+    return received.reshape(-1, LANES)
+
+
+def phase_body(pair_map, cotangent, conv_one, conv_two, norm_gain, norm_shift):
+    devices = lax.axis_size("row") * lax.axis_size("col")
+    residues = float(pair_map.shape[0] * lax.axis_size("row"))
+    table = phase_table(devices)
+    share = ROWS * 9 // 8 // devices
+    whole, line = (ROWS, LANES), (1, LANES)
+    part = functools.partial
+    me = lax.axis_index("row") * lax.axis_size("col") + lax.axis_index("col")
+    slot = lax.broadcasted_iota(jnp.int32, (SLOTS, LANES), 0)
+    own = ((slot % 4 == 3) & (me < DILATION_STEP // 2)).astype(jnp.float32)
+
+    (send,) = call(part(first_kernel, table), [whole], [whole])(pair_map)
+    x = exchange(send, devices)
+    hidden, send = call(
+        part(conv_one_kernel, table), [whole, (devices * (SLOTS + 1), LANES)], [whole]
+    )(x, conv_one, cotangent)
+    grad_recv = exchange(send, devices)
+    normed_one, inverse_one, active, second, send = call(
+        part(conv_two_kernel, devices), [whole, line, whole, whole, (devices, LANES)]
+    )(grad_recv, hidden, conv_two, norm_gain, norm_shift)
+    recv = exchange(send, devices)
+    normed_two, inverse_two, grad_sum, send = call(
+        part(output_kernel, devices), [whole, line, whole, (devices * (SLOTS + 1), LANES)]
+    )(recv, second, x, grad_recv, norm_gain, norm_shift, own)
+    sym_recv = exchange(send, devices)
+    grad_before, total_two, send = call(
+        part(back_two_kernel, devices),
+        [whole, line, (devices * (share + 1), LANES)],
+        [(devices * share, LANES)],
+    )(
+        sym_recv, grad_sum, normed_two, inverse_two, active, normed_one, conv_two,
+        norm_gain, norm_shift,
+    )
+    recv = exchange(send, devices)
+    total_one, kernel_two, send = call(
+        part(back_one_kernel, devices),
+        [line, (share, LANES), (devices * (share + SLOTS), LANES)],
+        [(devices * share, LANES)],
+    )(recv, grad_before, normed_one, inverse_one, x, grad_sum, conv_one, norm_gain)
+    map_recv = exchange(send, devices)
+    (send,) = call(part(share_kernel, devices), [(2 * devices * share, LANES)])(
+        map_recv, kernel_two
+    )
+    recv = exchange(send, devices)
+    taps = conv_one.shape[0] * conv_one.shape[1]
+    sym_out, grad_map, grad_one, grad_two, grad_gain, grad_shift = call(
+        part(last_kernel, table, residues),
+        [
+            pair_map.shape, pair_map.shape, (taps, HALF, HALF), (taps, HALF, HALF),
+            norm_gain.shape, norm_shift.shape,
+        ],
+        [whole, (devices * share, LANES)],
+    )(sym_recv, map_recv, recv, total_one, total_two)
+    return (
+        sym_out,
+        grad_map,
+        grad_one.reshape(conv_one.shape),
+        grad_two.reshape(conv_two.shape),
+        grad_gain,
+        grad_shift,
+    )
+
+
+def body(pair_map, cotangent, conv_one, conv_two, norm_gain, norm_shift):
+    devices = lax.axis_size("row") * lax.axis_size("col")
+    fits = (
+        conv_one.shape == (3, 3, HALF, HALF)
+        and pair_map.shape == (DILATION_STEP, 2 * DILATION_STEP * HALF)
+        and lax.axis_size("row") == SLOTS
+        and lax.axis_size("col") == 4
+    )
+    plan = phase_body if fits else general_body
+    return plan(pair_map, cotangent, conv_one, conv_two, norm_gain, norm_shift)
+
+
 def solution(mesh):
     return jax.shard_map(
         body,

time: 589 us -> 110 us (0.19)
  blocking collectives: 249 us -> 67.5 us
  waiting for transfers between devices: 153 us -> 15 us
  starting transfers between devices: 65.4 us -> 5.12 us
  local copies, waits for them, and re-layouts: 61 us -> 1.26 us
  other arithmetic: 30.9 us -> 0.68 us
  Pallas kernels: 0 us -> 19.5 us
  between operations: 15 us -> 0.68 us
  matrix products: 11.9 us -> 0 us
    psum x6 -> x0, blocking collectives: 249 us -> none  [the longest x2 85.4 us: normalize_back(): lax.psum((jnp.sum(grad_normed, axis=(0, 1)), jnp.sum(grad_normed * normed...]
    psum x1 -> x0, waiting for transfers between devices: 124 us -> none  [body(): total_one, total_two = lax.psum((kernel_one, kernel_two), ('row', 'col'))]
    all_to_all x0 -> x5, blocking collectives: none -> 67.5 us  [exchange(): lax.all_to_all(sent, AXES, split_axis=0, concat_axis=0, tiled=True)]
    ppermute x16 -> x0, starting transfers between devices: 41.1 us -> none  [the longest x8 30.5 us: extended_2(): lax.ppermute(tail, axis, [(i, (i + 1) % count) for i in range(ends)])]
    ppermute x16 -> x0, waiting for transfers between devices: 26.5 us -> none  [the longest x8 13.7 us: extended_2(): lax.ppermute(head, axis, [((i + 1) % count, i) for i in range(ends)])]
    unnamed x132 -> x4, local copies, waits for them, and re-layouts: 25 us -> 1.26 us
    pallas_call x0 -> x8, Pallas kernels: none -> 19.5 us  [the longest x1 3.27 us: phase_body(): call(part(back_one_kernel, devices), [line, (share, LANES), (devices * (s...]
    all_to_all x6 -> x2, starting transfers between devices: 24.3 us -> 5.12 us  [exchange(): lax.all_to_all(sent, AXES, split_axis=0, concat_axis=0, tiled=True)]
  transfers between devices with their start and end apart: 23 -> 2, of which waited for: 10 -> 2; matrix products, arithmetic and copies ran while one was open for 12% -> 1% of each run, Pallas kernels for 0% -> 0%
where the time goes in v1:
time: 110 us
  blocking collectives  67.5 us (61%)
  Pallas kernels  19.5 us (18%)
  waiting for transfers between devices  15 us (14%)
  starting transfers between devices  5.12 us (5%)
  local copies, waits for them, and re-layouts  1.26 us (1%)
    all_to_all x5, blocking collectives, exchange(): lax.all_to_all(sent, AXES, split_axis=0, concat_axis=0, tiled=True)  67.5 us
    all_to_all x2, waiting for transfers between devices, exchange(): lax.all_to_all(sent, AXES, split_axis=0, concat_axis=0, tiled=True)  15 us
    all_to_all x2, starting transfers between devices, exchange(): lax.all_to_all(sent, AXES, split_axis=0, concat_axis=0, tiled=True)  5.12 us
    pallas_call x1, Pallas kernels, phase_body(): call(part(back_one_kernel, devices), [line, (share, LANES), (devices * (s...  3.27 us
    pallas_call x1, Pallas kernels, phase_body(): call(part(back_two_kernel, devices), [whole, line, (devices * (share + 1)...  3.23 us
    pallas_call x1, Pallas kernels, phase_body(): call(part(conv_two_kernel, devices), [whole, line, whole, whole, (devices...  2.65 us
    pallas_call x1, Pallas kernels, phase_body(): call(part(conv_one_kernel, table), [whole, (devices * (SLOTS + 1), LANES)...  2.62 us
    pallas_call x1, Pallas kernels, phase_body(): call(part(last_kernel, table, residues), [pair_map.shape, pair_map.shape,...  2.26 us
  transfers between devices with their start and end apart: 2, of which 2 were waited for; matrix products, arithmetic and copies ran while one was open for 1% of the time, Pallas kernels for 0%

profile of v1, /device:TPU:0, one launch (start us, length us, event | category | flops | bytes accessed | tf_op | source)
XLA Modules:
  0.0 109.8 jit_solution(12353710182740588073)
XLA Ops:
  0.6 1.7 %shard_map.109 = f32[256,128]{1,0:T(8,128)} custom-call(f32[16,2048]{1,0:T(8,128)} %x_ref.1), custom_call_target="tpu_custom_call" | custom-call | tf_op jit(solution)/shard_map/pallas_call | solution.py:607
  2.3 15.8 %all_to_all.35 = f32[32,1,1024]{2,1,0:T(1,128)} all-to-all(f32[32,1,1024]{2,1,0:T(1,128)} %bitcast.30), channel_id=1, replica_groups=mesh['row'=8,'col'=4] {'row','col'}, dimensions={0} | all-to-all | bytes 262144 | tf_op jit(solution)/shard_map/all_to_all | solution.py:592
  18.2 2.6 %shard_map.110 = (f32[256,128]{1,0:T(8,128)}, f32[288,128]{1,0:T(8,128)}) custom-call(f32[256,128]{1,0:T(8,128)} %bitcast.20, f32[3,3,64,64]{3,2,1,0:T(8,128)} %weight_ref.7, f32[16,2048]{1,0:T(8,128)} %g_ref.1), custom_call_target="tpu_custom_call" | custom-call | tf_op jit(solution)/shard_map/pallas_call | solution.py:609
  20.8 2.6 %all-to-all-start.1 = ((f32[32,1,1152]{2,1,0:T(1,128)}), f32[32,1,1152]{2,1,0:T(1,128)S(1)}, u32[]{:S(2)}, u32[]{:S(2)}) async-start(f32[32,1,1152]{2,1,0:T(1,128)} %bitcast.33), calls=%async_computation.1 | async-start | bytes 294912 | tf_op jit(solution)/shard_map/all_to_all | solution.py:592
  23.4 8.6 %all-to-all-done.1 = f32[32,1,1152]{2,1,0:T(1,128)S(1)} async-done(((f32[32,1,1152]{2,1,0:T(1,128)}), f32[32,1,1152]{2,1,0:T(1,128)S(1)}, u32[]{:S(2)}, u32[]{:S(2)}) %all-to-all-start.1) | async-done | bytes 147488 | tf_op jit(solution)/shard_map/all_to_all | solution.py:592
  32.0 0.0 copy-start
  32.0 0.7 copy-done
  32.6 2.7 %shard_map.111 = (f32[256,128]{1,0:T(8,128)}, f32[1,128]{1,0:T(1,128)}, f32[256,128]{1,0:T(8,128)}, f32[256,128]{1,0:T(8,128)}, f32[32,128]{1,0:T(8,128)}) custom-call(f32[288,128]{1,0:T(8,128)} %bitcast.23, f32[256,128]{1,0:T(8,128)} %get-tuple-element.30.hidden_ref, f32[3,3,64,64]{3,2,1,0:T(8,128)} %weight_ref.6, f32[2,64]{1,0:T(2,128)} %gain_ref.7, ...), custom_call_target="tpu_custom_call" | custom-call | tf_op jit(solution)/shard_map/pallas_call | solution.py:613
  35.3 2.5 %all-to-all-start.2 = ((f32[32,1,128]{2,1,0:T(1,128)}), f32[32,1,128]{2,1,0:T(1,128)S(1)}, u32[]{:S(2)}, u32[]{:S(2)}) async-start(f32[32,1,128]{2,1,0:T(1,128)} %bitcast.36), calls=%async_computation.2 | async-start | bytes 32768 | tf_op jit(solution)/shard_map/all_to_all | solution.py:592
  37.8 0.7 fusion.1.own_ref
  38.5 6.5 %all-to-all-done.2 = f32[32,1,128]{2,1,0:T(1,128)S(1)} async-done(((f32[32,1,128]{2,1,0:T(1,128)}), f32[32,1,128]{2,1,0:T(1,128)S(1)}, u32[]{:S(2)}, u32[]{:S(2)}) %all-to-all-start.2) | async-done | bytes 16416 | tf_op jit(solution)/shard_map/all_to_all | solution.py:592
  45.0 0.0 copy-start.1
  45.0 0.6 copy-done.1
  45.6 2.0 %shard_map.112 = (f32[256,128]{1,0:T(8,128)}, f32[1,128]{1,0:T(1,128)}, f32[256,128]{1,0:T(8,128)}, f32[288,128]{1,0:T(8,128)}) custom-call(f32[32,128]{1,0:T(8,128)} %bitcast.35, f32[256,128]{1,0:T(8,128)} %get-tuple-element.32.second_ref, f32[256,128]{1,0:T(8,128)} %bitcast.21, f32[288,128]{1,0:T(8,128)} %bitcast.24, f32[2,64]{1,0:T(2,128)} %gain_ref.7, ...), custom_call_target="tpu_custom_call" | custom-call | tf_op jit(solution)/shard_map/pallas_call | solution.py:617
  47.6 11.9 %all_to_all.36 = f32[32,1,1152]{2,1,0:T(1,128)} all-to-all(f32[32,1,1152]{2,1,0:T(1,128)} %bitcast.34), channel_id=1, replica_groups=mesh['row'=8,'col'=4] {'row','col'}, dimensions={0} | all-to-all | bytes 294912 | tf_op jit(solution)/shard_map/all_to_all | solution.py:592
  59.5 3.2 %shard_map.113 = (f32[256,128]{1,0:T(8,128)}, f32[1,128]{1,0:T(1,128)}, f32[320,128]{1,0:T(8,128)}) custom-call(f32[288,128]{1,0:T(8,128)} %bitcast.25, f32[256,128]{1,0:T(8,128)} %get-tuple-element.34.sum_ref, f32[256,128]{1,0:T(8,128)} %get-tuple-element.35.normed_two_ref, f32[1,128]{1,0:T(1,128)} %get-tuple-element.36.inverse_two_ref, ...), custom_call_target="tpu_custom_call" | custom-call | tf_op jit(solution)/shard_map/pallas_call | solution.py:621
  62.7 12.1 %all_to_all.37 = f32[32,1,1280]{2,1,0:T(1,128)} all-to-all(f32[32,1,1280]{2,1,0:T(1,128)} %bitcast.32), channel_id=1, replica_groups=mesh['row'=8,'col'=4] {'row','col'}, dimensions={0} | all-to-all | bytes 327680 | tf_op jit(solution)/shard_map/all_to_all | solution.py:592
  74.8 3.3 %shard_map.114 = (f32[1,128]{1,0:T(1,128)}, f32[9,128]{1,0:T(8,128)}, f32[544,128]{1,0:T(8,128)}) custom-call(f32[320,128]{1,0:T(8,128)} %bitcast.29, f32[256,128]{1,0:T(8,128)} %get-tuple-element.40.before_ref, f32[256,128]{1,0:T(8,128)} %get-tuple-element.38.normed_ref, f32[1,128]{1,0:T(1,128)} %get-tuple-element.41.inverse_ref, f32[256,128]{1,0:T(8,128)} %bitcast.22, ...), custom_call_target="tpu_custom_call" | custom-call | tf_op jit(solution)/shard_map/pallas_call | solution.py:630
  78.1 13.7 %all_to_all.38 = f32[32,1,2176]{2,1,0:T(1,128)} all-to-all(f32[32,1,2176]{2,1,0:T(1,128)} %bitcast.31), channel_id=1, replica_groups=mesh['row'=8,'col'=4] {'row','col'}, dimensions={0} | all-to-all | bytes 557056 | tf_op jit(solution)/shard_map/all_to_all | solution.py:592
  91.8 1.7 %shard_map.115 = f32[576,128]{1,0:T(8,128)} custom-call(f32[544,128]{1,0:T(8,128)} %bitcast.18, f32[9,128]{1,0:T(8,128)} %get-tuple-element.43.two_ref), custom_call_target="tpu_custom_call" | custom-call | tf_op jit(solution)/shard_map/pallas_call | solution.py:636
  93.5 14.0 %all_to_all.39 = f32[32,1,2304]{2,1,0:T(1,128)} all-to-all(f32[32,1,2304]{2,1,0:T(1,128)} %bitcast.28), channel_id=1, replica_groups=mesh['row'=8,'col'=4] {'row','col'}, dimensions={0} | all-to-all | bytes 589824 | tf_op jit(solution)/shard_map/all_to_all | solution.py:592
  107.5 2.3 %shard_map.116 = (f32[16,2048]{1,0:T(8,128)}, f32[16,2048]{1,0:T(8,128)}, f32[9,64,64]{2,1,0:T(8,128)}, f32[9,64,64]{2,1,0:T(8,128)}, f32[2,64]{1,0:T(2,128)}, /*index=5*/f32[2,64]{1,0:T(2,128)}) custom-call(f32[288,128]{1,0:T(8,128)} %bitcast.26, f32[544,128]{1,0:T(8,128)} %bitcast.19, f32[576,128]{1,0:T(8,128)} %bitcast.27, ...), custom_call_target="tpu_custom_call" | custom-call | tf_op jit(solution)/shard_map/pallas_call | solution.py:641
  (2 shorter events, 0.0 us)
Async XLA Ops:
  20.8 11.2 %all-to-all-start.1 = ((f32[32,1,1152]{2,1,0:T(1,128)}), f32[32,1,1152]{2,1,0:T(1,128)S(1)}, u32[]{:S(2)}, u32[]{:S(2)}) async-start(f32[32,1,1152]{2,1,0:T(1,128)} %bitcast.33), calls=%async_computation.1 | async-start | bytes 294912 | tf_op jit(solution)/shard_map/all_to_all | solution.py:592
  32.0 0.7 copy-start
  35.3 9.7 %all-to-all-start.2 = ((f32[32,1,128]{2,1,0:T(1,128)}), f32[32,1,128]{2,1,0:T(1,128)S(1)}, u32[]{:S(2)}, u32[]{:S(2)}) async-start(f32[32,1,128]{2,1,0:T(1,128)} %bitcast.36), calls=%async_computation.2 | async-start | bytes 32768 | tf_op jit(solution)/shard_map/all_to_all | solution.py:592
  45.0 0.6 copy-start.1

commit v2 on v1

--- a/solution.py
+++ b/solution.py
@@ -211,6 +211,7 @@
 HALF = 64
 ROWS = 256
 AXES = ("row", "col")
+VMEM_BYTES = 8 << 20
 
 
 def phase_table(devices):
@@ -584,6 +585,7 @@
         body,
         out_shape=[jax.ShapeDtypeStruct(s, jnp.float32) for s in shapes],
         scratch_shapes=[pltpu.VMEM(s, jnp.float32) for s in scratch],
+        compiler_params=pltpu.CompilerParams(vmem_limit_bytes=VMEM_BYTES),
     )
 
 

time: 110 us -> 92.8 us (0.84)
  Pallas kernels: 19.5 us -> 7.24 us
  blocking collectives: 67.5 us -> 61.9 us
    all_to_all x5, blocking collectives: 67.5 us -> 61.9 us  [exchange(): lax.all_to_all(sent, AXES, split_axis=0, concat_axis=0, tiled=True)]
    pallas_call x1, Pallas kernels: 3.27 us -> 1.27 us  [phase_body(): call(part(back_one_kernel, devices), [line, (share, LANES), (devices * (s...]
    pallas_call x1, Pallas kernels: 3.23 us -> 1.26 us  [phase_body(): call(part(back_two_kernel, devices), [whole, line, (devices * (share + 1)...]
    pallas_call x1, Pallas kernels: 2.02 us -> 0.28 us  [phase_body(): call(part(output_kernel, devices), [whole, line, whole, (devices * (SLOTS...]
    pallas_call x1, Pallas kernels: 1.72 us -> 0.05 us  [phase_body(): call(part(share_kernel, devices), [(2 * devices * share, LANES)])]
    pallas_call x1, Pallas kernels: 1.7 us -> 0.14 us  [phase_body(): send, = call(part(first_kernel, table), [whole], [whole])(pair_map)]
    pallas_call x1, Pallas kernels: 2.65 us -> 1.53 us  [phase_body(): call(part(conv_two_kernel, devices), [whole, line, whole, whole, (devices...]
    pallas_call x1, Pallas kernels: 2.26 us -> 1.15 us  [phase_body(): call(part(last_kernel, table, residues), [pair_map.shape, pair_map.shape,...]
  transfers between devices with their start and end apart: 2 -> 2, of which waited for: 2 -> 2; matrix products, arithmetic and copies ran while one was open for 1% -> 0% of each run, Pallas kernels for 0% -> 0%
where the time goes in v2:
time: 92.8 us; the launch traced here: 92.4 us
  blocking collectives  61.9 us (67%)
  waiting for transfers between devices  15.6 us (17%)
  Pallas kernels  7.24 us (8%)
  starting transfers between devices  5.25 us (6%)
  local copies, waits for them, and re-layouts  1.64 us (2%)
    all_to_all x5, blocking collectives, exchange(): lax.all_to_all(sent, AXES, split_axis=0, concat_axis=0, tiled=True)  61.9 us
    all_to_all x2, waiting for transfers between devices, exchange(): lax.all_to_all(sent, AXES, split_axis=0, concat_axis=0, tiled=True)  15.6 us
    all_to_all x2, starting transfers between devices, exchange(): lax.all_to_all(sent, AXES, split_axis=0, concat_axis=0, tiled=True)  5.25 us
  transfers between devices with their start and end apart: 2, of which 2 were waited for; matrix products, arithmetic and copies ran while one was open for 0% of the time, Pallas kernels for 0%

profile of v2, /device:TPU:0, one launch (start us, length us, event | category | flops | bytes accessed | tf_op | source)
XLA Modules:
  0.0 92.4 jit_solution(2464338388353722255)
XLA Ops:
  0.6 0.0 copy-start.1
  0.6 0.0 copy-start.3
  0.7 0.9 %copy-done.3 = f32[16,2048]{1,0:T(8,128)S(1)} copy-done((f32[16,2048]{1,0:T(8,128)S(1)}, f32[16,2048]{1,0:T(8,128)}, u32[]{:S(2)}) %copy-start.3) | copy-done | bytes 131096
  1.6 0.1 shard_map.109
  1.7 0.0 copy-start.2
  1.8 15.5 %all_to_all.35 = f32[32,1,1024]{2,1,0:T(1,128)S(1)} all-to-all(f32[32,1,1024]{2,1,0:T(1,128)S(1)} %bitcast.30), channel_id=1, replica_groups=mesh['row'=8,'col'=4] {'row','col'}, dimensions={0} | all-to-all | bytes 262144 | tf_op jit(solution)/shard_map/all_to_all | solution.py:594
  17.3 0.0 copy-done.1
  17.3 0.0 copy-done.2
  17.3 1.6 %shard_map.110 = (f32[256,128]{1,0:T(8,128)S(1)}, f32[288,128]{1,0:T(8,128)}) custom-call(f32[256,128]{1,0:T(8,128)S(1)} %bitcast.20, f32[3,3,64,64]{3,2,1,0:T(8,128)S(1)} %copy-done.1, f32[16,2048]{1,0:T(8,128)S(1)} %copy-done.2), custom_call_target="tpu_custom_call" | custom-call | tf_op jit(solution)/shard_map/pallas_call | solution.py:611
  18.8 0.0 copy-start
  18.8 2.7 %all-to-all-start.1 = ((f32[32,1,1152]{2,1,0:T(1,128)}), f32[32,1,1152]{2,1,0:T(1,128)S(1)}, u32[]{:S(2)}, u32[]{:S(2)}) async-start(f32[32,1,1152]{2,1,0:T(1,128)} %bitcast.2), calls=%async_computation.1 | async-start | bytes 294912 | tf_op jit(solution)/shard_map/all_to_all | solution.py:594
  21.6 0.0 copy-start.5
  21.6 8.6 %all-to-all-done.1 = f32[32,1,1152]{2,1,0:T(1,128)S(1)} async-done(((f32[32,1,1152]{2,1,0:T(1,128)}), f32[32,1,1152]{2,1,0:T(1,128)S(1)}, u32[]{:S(2)}, u32[]{:S(2)}) %all-to-all-start.1) | async-done | bytes 147488 | tf_op jit(solution)/shard_map/all_to_all | solution.py:594
  30.2 0.0 copy-start.4
  30.2 0.0 copy-done
  30.2 0.0 copy-done.5
  30.2 0.7 copy-done.4
  30.8 1.5 %shard_map.111 = (f32[256,128]{1,0:T(8,128)S(1)}, f32[1,128]{1,0:T(1,128)S(1)}, f32[256,128]{1,0:T(8,128)S(1)}, f32[256,128]{1,0:T(8,128)S(1)}, f32[32,128]{1,0:T(8,128)}) custom-call(f32[288,128]{1,0:T(8,128)S(1)} %bitcast.23, f32[256,128]{1,0:T(8,128)S(1)} %get-tuple-element.30.hidden_ref, f32[3,3,64,64]{3,2,1,0:T(8,128)S(1)} %copy-done, ...), custom_call_target="tpu_custom_call" | custom-call | tf_op jit(solution)/shard_map/pallas_call | solution.py:615
  32.4 2.5 %all-to-all-start.2 = ((f32[32,1,128]{2,1,0:T(1,128)}), f32[32,1,128]{2,1,0:T(1,128)S(1)}, u32[]{:S(2)}, u32[]{:S(2)}) async-start(f32[32,1,128]{2,1,0:T(1,128)} %bitcast.5), calls=%async_computation.2 | async-start | bytes 32768 | tf_op jit(solution)/shard_map/all_to_all | solution.py:594
  34.9 0.1 fusion.1.own_ref
  35.0 7.0 %all-to-all-done.2 = f32[32,1,128]{2,1,0:T(1,128)S(1)} async-done(((f32[32,1,128]{2,1,0:T(1,128)}), f32[32,1,128]{2,1,0:T(1,128)S(1)}, u32[]{:S(2)}, u32[]{:S(2)}) %all-to-all-start.2) | async-done | bytes 16416 | tf_op jit(solution)/shard_map/all_to_all | solution.py:594
  42.1 0.3 shard_map.112
  42.3 10.3 %all_to_all.36 = f32[32,1,1152]{2,1,0:T(1,128)S(1)} all-to-all(f32[32,1,1152]{2,1,0:T(1,128)S(1)} %bitcast.33), channel_id=1, replica_groups=mesh['row'=8,'col'=4] {'row','col'}, dimensions={0} | all-to-all | bytes 294912 | tf_op jit(solution)/shard_map/all_to_all | solution.py:594
  52.7 1.3 %shard_map.113 = (f32[256,128]{1,0:T(8,128)S(1)}, f32[1,128]{1,0:T(1,128)S(1)}, f32[320,128]{1,0:T(8,128)S(1)}) custom-call(f32[288,128]{1,0:T(8,128)S(1)} %bitcast.25, f32[256,128]{1,0:T(8,128)S(1)} %get-tuple-element.34.sum_ref, f32[256,128]{1,0:T(8,128)S(1)} %get-tuple-element.35.normed_two_ref, f32[1,128]{1,0:T(1,128)S(1)} %get-tuple-element.36.inverse_two_ref, ...), custom_call_target="tpu_custom_call" | custom-call | tf_op jit(solution)/shard_map/pallas_call | solution.py:623
  53.9 10.6 %all_to_all.37 = f32[32,1,1280]{2,1,0:T(1,128)S(1)} all-to-all(f32[32,1,1280]{2,1,0:T(1,128)S(1)} %bitcast.32), channel_id=1, replica_groups=mesh['row'=8,'col'=4] {'row','col'}, dimensions={0} | all-to-all | bytes 327680 | tf_op jit(solution)/shard_map/all_to_all | solution.py:594
  64.5 1.3 %shard_map.114 = (f32[1,128]{1,0:T(1,128)S(1)}, f32[9,128]{1,0:T(8,128)S(1)}, f32[544,128]{1,0:T(8,128)S(1)}) custom-call(f32[320,128]{1,0:T(8,128)S(1)} %bitcast.29, f32[256,128]{1,0:T(8,128)S(1)} %get-tuple-element.40.before_ref, f32[256,128]{1,0:T(8,128)S(1)} %get-tuple-element.38.normed_ref, f32[1,128]{1,0:T(1,128)S(1)} %get-tuple-element.41.inverse_ref, ...), custom_call_target="tpu_custom_call" | custom-call | tf_op jit(solution)/shard_map/pallas_call | solution.py:632
  65.7 12.2 %all_to_all.38 = f32[32,1,2176]{2,1,0:T(1,128)S(1)} all-to-all(f32[32,1,2176]{2,1,0:T(1,128)S(1)} %bitcast.31), channel_id=1, replica_groups=mesh['row'=8,'col'=4] {'row','col'}, dimensions={0} | all-to-all | bytes 557056 | tf_op jit(solution)/shard_map/all_to_all | solution.py:594
  77.9 0.1 shard_map.115
  78.0 13.3 %all_to_all.39 = f32[32,1,2304]{2,1,0:T(1,128)S(1)} all-to-all(f32[32,1,2304]{2,1,0:T(1,128)S(1)} %bitcast.28), channel_id=1, replica_groups=mesh['row'=8,'col'=4] {'row','col'}, dimensions={0} | all-to-all | bytes 589824 | tf_op jit(solution)/shard_map/all_to_all | solution.py:594
  91.3 1.1 %shard_map.116 = (f32[16,2048]{1,0:T(8,128)}, f32[16,2048]{1,0:T(8,128)}, f32[9,64,64]{2,1,0:T(8,128)}, f32[9,64,64]{2,1,0:T(8,128)}, f32[2,64]{1,0:T(2,128)}, /*index=5*/f32[2,64]{1,0:T(2,128)}) custom-call(f32[288,128]{1,0:T(8,128)S(1)} %bitcast.26, f32[544,128]{1,0:T(8,128)S(1)} %bitcast.19, f32[576,128]{1,0:T(8,128)S(1)} %bitcast.27, ...), custom_call_target="tpu_custom_call" | custom-call | tf_op jit(solution)/shard_map/pallas_call | solution.py:643
  (2 shorter events, 0.0 us)
Async XLA Ops:
  0.6 16.6 %copy-start.1 = (f32[3,3,64,64]{3,2,1,0:T(8,128)S(1)}, f32[3,3,64,64]{3,2,1,0:T(8,128)}, u32[]{:S(2)}) copy-start(f32[3,3,64,64]{3,2,1,0:T(8,128)} %weight_ref.7) | copy-start | bytes 442372
  0.6 0.9 %copy-start.3 = (f32[16,2048]{1,0:T(8,128)S(1)}, f32[16,2048]{1,0:T(8,128)}, u32[]{:S(2)}) copy-start(f32[16,2048]{1,0:T(8,128)} %x_ref.1) | copy-start | bytes 393220
  1.7 15.5 %copy-start.2 = (f32[16,2048]{1,0:T(8,128)S(1)}, f32[16,2048]{1,0:T(8,128)}, u32[]{:S(2)}) copy-start(f32[16,2048]{1,0:T(8,128)} %g_ref.1) | copy-start | bytes 393220
  18.8 11.3 %copy-start = (f32[3,3,64,64]{3,2,1,0:T(8,128)S(1)}, f32[3,3,64,64]{3,2,1,0:T(8,128)}, u32[]{:S(2)}) copy-start(f32[3,3,64,64]{3,2,1,0:T(8,128)} %weight_ref.6) | copy-start | bytes 442372
  18.8 11.3 %all-to-all-start.1 = ((f32[32,1,1152]{2,1,0:T(1,128)}), f32[32,1,1152]{2,1,0:T(1,128)S(1)}, u32[]{:S(2)}, u32[]{:S(2)}) async-start(f32[32,1,1152]{2,1,0:T(1,128)} %bitcast.2), calls=%async_computation.1 | async-start | bytes 294912 | tf_op jit(solution)/shard_map/all_to_all | solution.py:594
  21.6 8.6 %copy-start.5 = (f32[2,64]{1,0:T(2,128)S(1)}, f32[2,64]{1,0:T(2,128)}, u32[]{:S(2)}) copy-start(f32[2,64]{1,0:T(2,128)} %shift_ref.5) | copy-start | bytes 1540
  30.2 0.7 copy-start.4
  32.4 9.7 %all-to-all-start.2 = ((f32[32,1,128]{2,1,0:T(1,128)}), f32[32,1,128]{2,1,0:T(1,128)S(1)}, u32[]{:S(2)}, u32[]{:S(2)}) async-start(f32[32,1,128]{2,1,0:T(1,128)} %bitcast.5), calls=%async_computation.2 | async-start | bytes 32768 | tf_op jit(solution)/shard_map/all_to_all | solution.py:594

commit v3 on v2

--- a/solution.py
+++ b/solution.py
@@ -212,6 +212,7 @@
 ROWS = 256
 AXES = ("row", "col")
 VMEM_BYTES = 8 << 20
+TAP_SOURCES = ((1, 2), (2, 3), (3, 0))
 
 
 def phase_table(devices):
@@ -354,18 +355,58 @@
     )
 
 
-def kernel_rows(joined, grad):
-    product = exact_dot(joined, spread_shifts(grad), ((0,), (0,)))
+def tap_rows(product):
+    low = lane_low((HALF // 2, LANES))
     pieces = []
     for a in range(3):
         part = product[:, a * LANES : (a + 1) * LANES]
-        for even, odd in ((1, 2), (2, 3), (3, 0)):
+        for even, odd in TAP_SOURCES:
             tap = part[even * HALF : (even + 1) * HALF] + swap_halves(
                 part[odd * HALF : (odd + 1) * HALF]
             )
-            low = lane_low((HALF // 2, LANES))
             pieces.append(jnp.where(low, tap[: HALF // 2], swap_halves(tap[HALF // 2 :])))
     return jnp.concatenate(pieces, axis=0)
+
+
+def kernel_rows(joined, grad):
+    return tap_rows(exact_dot(joined, spread_shifts(grad), ((0,), (0,))))
+
+
+def kernel_rows_and_sums(joined, grad, devices):
+    row = lax.broadcasted_iota(jnp.int32, (ROWS, LANES), 0)
+    tap = (lax.broadcasted_iota(jnp.int32, (ROWS, LANES), 1) % HALF) % 3
+    step = 4 * SLOTS
+    outside = ((tap == 0) & (row >= ROWS - step)) | ((tap == 2) & (row < step))
+    ones = jnp.where(outside, 0.0, 1.0)
+    product = exact_dot(
+        joined, jnp.concatenate([spread_shifts(grad), ones], axis=1), ((0,), (0,))
+    )
+    part = product[:, 3 * LANES :]
+    low = lane_low((HALF // 2, LANES))
+    pieces = []
+    for even, odd in TAP_SOURCES:
+        both = part[even * HALF : (even + 1) * HALF] + part[odd * HALF : (odd + 1) * HALF]
+        pieces.append(jnp.where(low, both[: HALF // 2], both[HALF // 2 :]))
+    sums = jnp.concatenate(pieces * 3, axis=0)
+    total = sums.shape[0]
+    share = total // devices
+    row = lax.broadcasted_iota(jnp.int32, (total, LANES), 0)
+    lane = lax.broadcasted_iota(jnp.int32, (total, LANES), 1) % HALF
+    sums = jnp.where(lane == 3 * (row % share) + row // (total // 3), sums, 0.0)
+    owner = lax.broadcasted_iota(jnp.int32, (devices, total), 0)
+    index = lax.broadcasted_iota(jnp.int32, (devices, total), 1)
+    picked = (index // share == owner).astype(jnp.float32)
+    return tap_rows(product), exact_dot(picked, sums, ((1,), (0,)))
+
+
+def widen_sums(row, share):
+    lane = lax.broadcasted_iota(jnp.int32, (share, LANES), 1)
+    index = lax.broadcasted_iota(jnp.int32, (share, LANES), 0)
+    picked = jnp.where((lane % HALF) // 3 == index, row, 0.0)
+    low = lane < HALF
+    first = jnp.sum(jnp.where(low, picked, 0.0), axis=1, keepdims=True)
+    second = jnp.sum(jnp.where(low, 0.0, picked), axis=1, keepdims=True)
+    return jnp.where(low, first, second)
 
 
 def local_stats(hidden):
@@ -423,55 +464,77 @@
     return jnp.concatenate(pieces, axis=0)
 
 
-def first_kernel(table, x_ref, send_ref, scratch_ref):
+def own_mirrors():
+    me = lax.axis_index("row") * lax.axis_size("col") + lax.axis_index("col")
+    slot = lax.broadcasted_iota(jnp.int32, (SLOTS, LANES), 0)
+    return (slot % 4 == 3) & (me < DILATION_STEP // 2)
+
+
+def first_kernel(
+    table, x_ref, g_ref, gain_ref, shift_ref, send_ref, grad_ref, affine_ref, scratch_ref, other_ref
+):
     split_phases(x_ref, scratch_ref)
     pack_rows(table, scratch_ref, send_ref, SLOTS)
-
-
-def conv_one_kernel(table, x_ref, weight_ref, g_ref, hidden_ref, send_ref, scratch_ref):
-    split_phases(g_ref, scratch_ref)
+    split_phases(g_ref, other_ref)
+    pack_rows(table, other_ref, grad_ref, SLOTS)
+    affine_ref[...] = jnp.concatenate(
+        [twice(gain_ref[...]), twice(shift_ref[...]), jnp.zeros((4, LANES), jnp.float32)], axis=0
+    )
+
+
+def conv_one_kernel(devices, x_ref, weight_ref, g_ref, hidden_ref, send_ref):
     stride = SLOTS + 1
-    pack_rows(table, scratch_ref, send_ref, stride)
     hidden = shifted_sum(
         exact_dot(neighbours(x_ref[...]), forward_weight(weight_ref), ((1,), (0,)))
     )
     hidden_ref[...] = hidden
     stats = local_stats(hidden)
-    for d in range(len(table)):
+    for d in range(devices):
+        send_ref[d * stride : d * stride + SLOTS, :] = g_ref[d * SLOTS : (d + 1) * SLOTS, :]
         send_ref[d * stride + SLOTS : (d + 1) * stride, :] = stats
 
 
 def conv_two_kernel(
-    devices, recv_ref, hidden_ref, weight_ref, gain_ref, shift_ref,
-    normed_ref, inverse_ref, active_ref, second_ref, send_ref,
+    devices, recv_ref, hidden_ref, x_ref, weight_ref, affine_ref,
+    normed_ref, inverse_ref, active_ref, second_ref, send_ref, scratch_ref,
 ):
-    stride = SLOTS + 1
-    mean, inverse = combine_stats(recv_ref[pl.ds(SLOTS, devices, stride=stride), :], devices)
+    mean, inverse = combine_stats(recv_ref[pl.ds(SLOTS, devices, stride=SLOTS + 1), :], devices)
     normed = (hidden_ref[...] - mean) * inverse
     normed_ref[...] = normed
     inverse_ref[...] = inverse
-    active = elu_value(normed * twice(gain_ref[0:1, :]) + twice(shift_ref[0:1, :]))
+    active = elu_value(normed * affine_ref[0:1, :] + affine_ref[2:3, :])
     active_ref[...] = active
     second = shifted_sum(
         exact_dot(neighbours(active), forward_weight(weight_ref), ((1,), (0,)))
     )
     second_ref[...] = second
-    send_ref[...] = jnp.broadcast_to(local_stats(second), (devices, LANES))
+    stats = local_stats(second)
+    rows, sums = kernel_rows_and_sums(neighbours(x_ref[...]), normed, devices)
+    scratch_ref[...] = rows
+    share = rows.shape[0] // devices
+    stride = share + 2
+    for d in range(devices):
+        begin = d * stride
+        send_ref[begin : begin + share, :] = scratch_ref[d * share : (d + 1) * share, :]
+        send_ref[begin + share : begin + share + 1, :] = sums[d : d + 1, :]
+        send_ref[begin + share + 1 : begin + stride, :] = stats
 
 
 def output_kernel(
-    devices, recv_ref, second_ref, x_ref, grad_ref, gain_ref, shift_ref, own_ref,
+    devices, share, recv_ref, second_ref, x_ref, grad_ref, affine_ref,
     normed_ref, inverse_ref, sum_ref, send_ref,
 ):
     stride = SLOTS + 1
-    mean, inverse = combine_stats(recv_ref[...], devices)
+    mean, inverse = combine_stats(
+        recv_ref[pl.ds(share + 1, devices, stride=share + 2), :], devices
+    )
     normed = (second_ref[...] - mean) * inverse
     normed_ref[...] = normed
     inverse_ref[...] = inverse
-    summed = x_ref[...] + normed * twice(gain_ref[1:2, :]) + twice(shift_ref[1:2, :])
+    summed = x_ref[...] + normed * affine_ref[1:2, :] + affine_ref[3:4, :]
     slope = jnp.exp(jnp.minimum(summed, 0.0))
     out = jnp.where(summed > 0, summed, slope - 1.0)
-    own = own_ref[...] > 0
+    own = own_mirrors()
     symmetric = 0.5 * (out + mirrored(out, own))
     for d in range(devices):
         send_ref[d * stride : d * stride + SLOTS, :] = symmetric[d * SLOTS : (d + 1) * SLOTS]
@@ -485,93 +548,87 @@
 
 
 def back_two_kernel(
-    devices, recv_ref, sum_ref, normed_two_ref, inverse_two_ref, active_ref, normed_ref,
-    weight_ref, gain_ref, shift_ref, before_ref, total_ref, send_ref, scratch_ref,
+    devices, share, recv_ref, sum_ref, normed_two_ref, inverse_two_ref, active_ref, normed_ref,
+    x_ref, weight_ref, affine_ref, before_ref, total_ref, send_ref, two_ref, one_ref,
 ):
     cells = 2.0 * ROWS * devices
     shift_sum, gain_sum = split_sums(recv_ref[pl.ds(SLOTS, devices, stride=SLOTS + 1), :])
     total_ref[...] = jnp.where(lane_low((1, LANES)), shift_sum, gain_sum)
     grad_second = norm_back(
-        sum_ref[...], normed_two_ref[...], inverse_two_ref[...], twice(gain_ref[1:2, :]),
+        sum_ref[...], normed_two_ref[...], inverse_two_ref[...], affine_ref[1:2, :],
         shift_sum, gain_sum, cells,
     )
     grad_active = shifted_sum(
         exact_dot(neighbours(grad_second), backward_weight(weight_ref), ((1,), (1,)))
     )
     normed = normed_ref[...]
-    before = normed * twice(gain_ref[0:1, :]) + twice(shift_ref[0:1, :])
+    before = normed * affine_ref[0:1, :] + affine_ref[2:3, :]
     grad_before = grad_active * jnp.where(before > 0, 1.0, jnp.exp(jnp.minimum(before, 0.0)))
     before_ref[...] = grad_before
     sums = pair_sums(grad_before, normed)
-    share = ROWS * 9 // 8 // devices
-    stride = share + 1
-    scratch_ref[...] = kernel_rows(neighbours(active_ref[...]), grad_second)
+    two_ref[...] = kernel_rows(neighbours(active_ref[...]), grad_second)
+    one_ref[...] = kernel_rows(neighbours(x_ref[...]), grad_before)
+    stride = 2 * share + 1
     for d in range(devices):
-        send_ref[d * stride : d * stride + share, :] = scratch_ref[d * share : (d + 1) * share, :]
-        send_ref[d * stride + share : (d + 1) * stride, :] = sums
-
-
-def reduce_share(ref, devices, share, stride):
-    total = ref[0:share, :]
+        begin = d * stride
+        send_ref[begin : begin + share, :] = one_ref[d * share : (d + 1) * share, :]
+        send_ref[begin + share : begin + 2 * share, :] = two_ref[d * share : (d + 1) * share, :]
+        send_ref[begin + 2 * share : begin + stride, :] = sums
+
+
+def reduce_share(ref, devices, begin, size, stride):
+    total = ref[begin : begin + size, :]
     for d in range(1, devices):
-        total = total + ref[d * stride : d * stride + share, :]
+        total = total + ref[d * stride + begin : d * stride + begin + size, :]
     return total
 
 
 def back_one_kernel(
-    devices, recv_ref, before_ref, normed_ref, inverse_ref, x_ref, sum_ref, weight_ref, gain_ref,
-    total_ref, two_ref, send_ref, scratch_ref,
+    devices, share, residues, recv_ref, before_ref, normed_ref, inverse_ref, sum_ref, weight_ref,
+    affine_ref, normed_recv_ref, total_ref, send_ref,
 ):
     cells = 2.0 * ROWS * devices
-    share = ROWS * 9 // 8 // devices
-    stride = share + 1
-    shift_sum, gain_sum = split_sums(recv_ref[pl.ds(share, devices, stride=stride), :])
+    stride = 2 * share + 1
+    shift_sum, gain_sum = split_sums(recv_ref[pl.ds(2 * share, devices, stride=stride), :])
     total_ref[...] = jnp.where(lane_low((1, LANES)), shift_sum, gain_sum)
-    two_ref[...] = reduce_share(recv_ref, devices, share, stride)
+    gain, inverse = affine_ref[0:1, :], inverse_ref[...]
     grad_first = norm_back(
-        before_ref[...], normed_ref[...], inverse_ref[...], twice(gain_ref[0:1, :]),
-        shift_sum, gain_sum, cells,
+        before_ref[...], normed_ref[...], inverse, gain, shift_sum, gain_sum, cells
     )
     field = sum_ref[...] + shifted_sum(
         exact_dot(neighbours(grad_first), backward_weight(weight_ref), ((1,), (1,)))
     )
-    scratch_ref[...] = kernel_rows(neighbours(x_ref[...]), grad_first)
-    stride = share + SLOTS
+    one = reduce_share(recv_ref, devices, 0, share, stride)
+    two = reduce_share(recv_ref, devices, share, share, stride)
+    rows = reduce_share(normed_recv_ref, devices, 0, share + 1, share + 2)
+    constant = widen_sums(rows[share : share + 1], share)
+    one = (inverse * gain) * (
+        one - constant * (shift_sum / cells) - rows[:share] * (gain_sum / cells)
+    )
+    one, two = one / residues, two / residues
+    stride = 2 * share + SLOTS
     for d in range(devices):
-        send_ref[d * stride : d * stride + SLOTS, :] = field[d * SLOTS : (d + 1) * SLOTS]
-        send_ref[d * stride + SLOTS : (d + 1) * stride, :] = scratch_ref[
-            d * share : (d + 1) * share, :
-        ]
-
-
-def share_kernel(devices, recv_ref, two_ref, send_ref):
-    share = ROWS * 9 // 8 // devices
-    stride = share + SLOTS
-    total = recv_ref[SLOTS:stride, :]
-    for d in range(1, devices):
-        total = total + recv_ref[d * stride + SLOTS : (d + 1) * stride, :]
-    two = two_ref[...]
-    for d in range(devices):
-        send_ref[2 * d * share : (2 * d + 1) * share, :] = total
-        send_ref[(2 * d + 1) * share : (2 * d + 2) * share, :] = two
+        begin = d * stride
+        send_ref[begin : begin + SLOTS, :] = field[d * SLOTS : (d + 1) * SLOTS]
+        send_ref[begin + SLOTS : begin + SLOTS + share, :] = one
+        send_ref[begin + SLOTS + share : begin + stride, :] = two
 
 
 def last_kernel(
-    table, residues, sym_recv_ref, map_recv_ref, recv_ref, total_one_ref, total_two_ref,
+    table, share, residues, sym_recv_ref, recv_ref, total_one_ref, total_two_ref,
     sym_ref, map_ref, one_ref, two_ref, gain_ref, shift_ref, scratch_ref, rows_ref,
 ):
-    devices = len(table)
-    share = ROWS * 9 // 8 // devices
+    stride = 2 * share + SLOTS
     unpack_rows(table, sym_recv_ref, scratch_ref, SLOTS + 1, 0)
     join_phases(scratch_ref, sym_ref)
-    unpack_rows(table, map_recv_ref, scratch_ref, SLOTS + share, 0)
+    unpack_rows(table, recv_ref, scratch_ref, stride, 0)
     join_phases(scratch_ref, map_ref)
     for index, out_ref in ((0, one_ref), (1, two_ref)):
-        for d in range(devices):
-            begin = (2 * d + index) * share
+        for d in range(len(table)):
+            begin = d * stride + SLOTS + index * share
             rows_ref[d * share : (d + 1) * share, :] = recv_ref[begin : begin + share, :]
         for tap in range(9):
-            block = rows_ref[tap * HALF // 2 : (tap + 1) * HALF // 2, :] / residues
+            block = rows_ref[tap * HALF // 2 : (tap + 1) * HALF // 2, :]
             out_ref[tap, : HALF // 2, :] = block[:, :HALF]
             out_ref[tap, HALF // 2 :, :] = swap_halves(block)[:, :HALF]
     for index, total_ref in ((0, total_one_ref), (1, total_two_ref)):
@@ -600,54 +657,48 @@
     residues = float(pair_map.shape[0] * lax.axis_size("row"))
     table = phase_table(devices)
     share = ROWS * 9 // 8 // devices
-    whole, line = (ROWS, LANES), (1, LANES)
+    whole, line, rows = (ROWS, LANES), (1, LANES), (devices * share, LANES)
     part = functools.partial
-    me = lax.axis_index("row") * lax.axis_size("col") + lax.axis_index("col")
-    slot = lax.broadcasted_iota(jnp.int32, (SLOTS, LANES), 0)
-    own = ((slot % 4 == 3) & (me < DILATION_STEP // 2)).astype(jnp.float32)
-
-    (send,) = call(part(first_kernel, table), [whole], [whole])(pair_map)
+
+    def wide(count):
+        return (devices * count, LANES)
+
+    inputs = (pair_map, cotangent, norm_gain, norm_shift)
+    send, grad_sent, affine = call(
+        part(first_kernel, table), [whole, whole, (SLOTS, LANES)], [whole, whole]
+    )(*(pltpu.with_memory_space_constraint(v, pltpu.HBM) for v in inputs))
     x = exchange(send, devices)
-    hidden, send = call(
-        part(conv_one_kernel, table), [whole, (devices * (SLOTS + 1), LANES)], [whole]
-    )(x, conv_one, cotangent)
+    hidden, send = call(part(conv_one_kernel, devices), [whole, wide(SLOTS + 1)])(
+        x, conv_one, grad_sent
+    )
     grad_recv = exchange(send, devices)
     normed_one, inverse_one, active, second, send = call(
-        part(conv_two_kernel, devices), [whole, line, whole, whole, (devices, LANES)]
-    )(grad_recv, hidden, conv_two, norm_gain, norm_shift)
-    recv = exchange(send, devices)
+        part(conv_two_kernel, devices), [whole, line, whole, whole, wide(share + 2)], [rows]
+    )(grad_recv, hidden, x, conv_two, affine)
+    normed_recv = exchange(send, devices)
     normed_two, inverse_two, grad_sum, send = call(
-        part(output_kernel, devices), [whole, line, whole, (devices * (SLOTS + 1), LANES)]
-    )(recv, second, x, grad_recv, norm_gain, norm_shift, own)
+        part(output_kernel, devices, share), [whole, line, whole, wide(SLOTS + 1)]
+    )(normed_recv, second, x, grad_recv, affine)
     sym_recv = exchange(send, devices)
     grad_before, total_two, send = call(
-        part(back_two_kernel, devices),
-        [whole, line, (devices * (share + 1), LANES)],
-        [(devices * share, LANES)],
+        part(back_two_kernel, devices, share), [whole, line, wide(2 * share + 1)], [rows, rows]
     )(
-        sym_recv, grad_sum, normed_two, inverse_two, active, normed_one, conv_two,
-        norm_gain, norm_shift,
+        sym_recv, grad_sum, normed_two, inverse_two, active, normed_one, x, conv_two, affine
     )
     recv = exchange(send, devices)
-    total_one, kernel_two, send = call(
-        part(back_one_kernel, devices),
-        [line, (share, LANES), (devices * (share + SLOTS), LANES)],
-        [(devices * share, LANES)],
-    )(recv, grad_before, normed_one, inverse_one, x, grad_sum, conv_one, norm_gain)
-    map_recv = exchange(send, devices)
-    (send,) = call(part(share_kernel, devices), [(2 * devices * share, LANES)])(
-        map_recv, kernel_two
-    )
+    total_one, send = call(
+        part(back_one_kernel, devices, share, residues), [line, wide(2 * share + SLOTS)]
+    )(recv, grad_before, normed_one, inverse_one, grad_sum, conv_one, affine, normed_recv)
     recv = exchange(send, devices)
     taps = conv_one.shape[0] * conv_one.shape[1]
     sym_out, grad_map, grad_one, grad_two, grad_gain, grad_shift = call(
-        part(last_kernel, table, residues),
+        part(last_kernel, table, share, residues),
         [
             pair_map.shape, pair_map.shape, (taps, HALF, HALF), (taps, HALF, HALF),
             norm_gain.shape, norm_shift.shape,
         ],
-        [whole, (devices * share, LANES)],
-    )(sym_recv, map_recv, recv, total_one, total_two)
+        [whole, rows],
+    )(sym_recv, recv, total_one, total_two)
     return (
         sym_out,
         grad_map,

time: 92.8 us -> 84 us (0.905)
  waiting for transfers between devices: 15.6 us -> 0 us
  blocking collectives: 61.9 us -> 74.8 us
  starting transfers between devices: 5.25 us -> 0 us
  local copies, waits for them, and re-layouts: 1.64 us -> 0.01 us
    all_to_all x2 -> x0, waiting for transfers between devices: 15.6 us -> none  [exchange(): lax.all_to_all(sent, AXES, split_axis=0, concat_axis=0, tiled=True)]
    all_to_all x5 -> x6, blocking collectives: 61.9 us -> 74.8 us  [exchange(): lax.all_to_all(sent, AXES, split_axis=0, concat_axis=0, tiled=True)]
    all_to_all x2 -> x0, starting transfers between devices: 5.25 us -> none  [exchange(): lax.all_to_all(sent, AXES, split_axis=0, concat_axis=0, tiled=True)]
    unnamed x12 -> x4, local copies, waits for them, and re-layouts: 1.64 us -> 0.01 us
    pallas_call x8 -> x7, Pallas kernels: 7.24 us -> 7.36 us  [the longest x1 1.71 us: phase_body(): call(part(back_two_kernel, devices, share), [whole, line, wide(2 * share...]
  transfers between devices with their start and end apart: 2 -> 0, of which waited for: 2 -> 0; matrix products, arithmetic and copies ran while one was open for 0% -> 0% of each run, Pallas kernels for 0% -> 0%
where the time goes in v3:
time: 84 us; the launch traced here: 82.9 us
  blocking collectives  74.8 us (89%)
  Pallas kernels  7.36 us (9%)
    all_to_all x6, blocking collectives, exchange(): lax.all_to_all(sent, AXES, split_axis=0, concat_axis=0, tiled=True)  74.8 us
    pallas_call x1, Pallas kernels, phase_body(): call(part(back_two_kernel, devices, share), [whole, line, wide(2 * share...  1.71 us

profile of v3, /device:TPU:0, one launch (start us, length us, event | category | flops | bytes accessed | tf_op | source)
XLA Modules:
  0.0 82.9 jit_solution(17851054486472421463)
XLA Ops:
  0.6 0.0 copy-start
  0.6 1.2 %shard_map.109 = (f32[256,128]{1,0:T(8,128)S(1)}, f32[256,128]{1,0:T(8,128)S(1)}, f32[8,128]{1,0:T(8,128)S(1)}) custom-call(f32[16,2048]{1,0:T(8,128)} %x_ref.1, f32[16,2048]{1,0:T(8,128)} %g_ref.1, f32[2,64]{1,0:T(2,128)} %gain_ref.1, f32[2,64]{1,0:T(2,128)} %shift_ref.1), custom_call_target="tpu_custom_call" | custom-call | tf_op jit(solution)/shard_map/pallas_call | solution.py:667
  1.9 15.5 %all_to_all.30 = f32[32,1,1024]{2,1,0:T(1,128)S(1)} all-to-all(f32[32,1,1024]{2,1,0:T(1,128)S(1)} %bitcast.31), channel_id=1, replica_groups=mesh['row'=8,'col'=4] {'row','col'}, dimensions={0} | all-to-all | bytes 262144 | tf_op jit(solution)/shard_map/all_to_all | solution.py:651
  17.4 0.0 copy-done
  17.4 0.0 copy-start.1
  17.4 0.9 %shard_map.110 = (f32[256,128]{1,0:T(8,128)S(1)}, f32[288,128]{1,0:T(8,128)S(1)}) custom-call(f32[256,128]{1,0:T(8,128)S(1)} %bitcast.14, f32[3,3,64,64]{3,2,1,0:T(8,128)S(1)} %copy-done, f32[256,128]{1,0:T(8,128)S(1)} %get-tuple-element.32.g_ref), custom_call_target="tpu_custom_call" | custom-call | tf_op jit(solution)/shard_map/pallas_call | solution.py:671
  18.3 10.3 %all_to_all.31 = f32[32,1,1152]{2,1,0:T(1,128)S(1)} all-to-all(f32[32,1,1152]{2,1,0:T(1,128)S(1)} %bitcast.30), channel_id=1, replica_groups=mesh['row'=8,'col'=4] {'row','col'}, dimensions={0} | all-to-all | bytes 294912 | tf_op jit(solution)/shard_map/all_to_all | solution.py:651
  28.6 0.0 copy-done.1
  28.6 1.4 %shard_map.111 = (f32[256,128]{1,0:T(8,128)S(1)}, f32[1,128]{1,0:T(1,128)S(1)}, f32[256,128]{1,0:T(8,128)S(1)}, f32[256,128]{1,0:T(8,128)S(1)}, f32[352,128]{1,0:T(8,128)S(1)}) custom-call(f32[288,128]{1,0:T(8,128)S(1)} %bitcast.23, f32[256,128]{1,0:T(8,128)S(1)} %get-tuple-element.34.hidden_ref, f32[256,128]{1,0:T(8,128)S(1)} %bitcast.15, ...), custom_call_target="tpu_custom_call" | custom-call | tf_op jit(solution)/shard_map/pallas_call | solution.py:675
  30.0 10.8 %all_to_all.32 = f32[32,1,1408]{2,1,0:T(1,128)S(1)} all-to-all(f32[32,1,1408]{2,1,0:T(1,128)S(1)} %bitcast.28), channel_id=1, replica_groups=mesh['row'=8,'col'=4] {'row','col'}, dimensions={0} | all-to-all | bytes 360448 | tf_op jit(solution)/shard_map/all_to_all | solution.py:651
  40.8 0.3 shard_map.112
  41.1 10.5 %all_to_all.33 = f32[32,1,1152]{2,1,0:T(1,128)S(1)} all-to-all(f32[32,1,1152]{2,1,0:T(1,128)S(1)} %bitcast.29), channel_id=1, replica_groups=mesh['row'=8,'col'=4] {'row','col'}, dimensions={0} | all-to-all | bytes 294912 | tf_op jit(solution)/shard_map/all_to_all | solution.py:651
  51.5 1.7 %shard_map.113 = (f32[256,128]{1,0:T(8,128)S(1)}, f32[1,128]{1,0:T(1,128)S(1)}, f32[608,128]{1,0:T(8,128)S(1)}) custom-call(f32[288,128]{1,0:T(8,128)S(1)} %bitcast.21, f32[256,128]{1,0:T(8,128)S(1)} %get-tuple-element.39.sum_ref, f32[256,128]{1,0:T(8,128)S(1)} %get-tuple-element.40.normed_two_ref, f32[1,128]{1,0:T(1,128)S(1)} %get-tuple-element.41.inverse_two_ref, ...), custom_call_target="tpu_custom_call" | custom-call | tf_op jit(solution)/shard_map/pallas_call | solution.py:683
  53.3 12.6 %all_to_all.34 = f32[32,1,2432]{2,1,0:T(1,128)S(1)} all-to-all(f32[32,1,2432]{2,1,0:T(1,128)S(1)} %bitcast.27), channel_id=1, replica_groups=mesh['row'=8,'col'=4] {'row','col'}, dimensions={0} | all-to-all | bytes 622592 | tf_op jit(solution)/shard_map/all_to_all | solution.py:651
  65.8 0.7 shard_map.114
  66.6 15.2 %all_to_all.35 = f32[32,1,3328]{2,1,0:T(1,128)S(1)} all-to-all(f32[32,1,3328]{2,1,0:T(1,128)S(1)} %bitcast.26), channel_id=1, replica_groups=mesh['row'=8,'col'=4] {'row','col'}, dimensions={0} | all-to-all | bytes 851968 | tf_op jit(solution)/shard_map/all_to_all | solution.py:651
  81.7 1.1 %shard_map.115 = (f32[16,2048]{1,0:T(8,128)}, f32[16,2048]{1,0:T(8,128)}, f32[9,64,64]{2,1,0:T(8,128)}, f32[9,64,64]{2,1,0:T(8,128)}, f32[2,64]{1,0:T(2,128)}, /*index=5*/f32[2,64]{1,0:T(2,128)}) custom-call(f32[288,128]{1,0:T(8,128)S(1)} %bitcast.22, f32[832,128]{1,0:T(8,128)S(1)} %bitcast.18, f32[1,128]{1,0:T(1,128)S(1)} %get-tuple-element.48.total_one_ref, ...), custom_call_target="tpu_custom_call" | custom-call | tf_op jit(solution)/shard_map/pallas_call | solution.py:694
Async XLA Ops:
  0.6 16.8 %copy-start = (f32[3,3,64,64]{3,2,1,0:T(8,128)S(1)}, f32[3,3,64,64]{3,2,1,0:T(8,128)}, u32[]{:S(2)}) copy-start(f32[3,3,64,64]{3,2,1,0:T(8,128)} %weight_ref.7) | copy-start | bytes 442372
  17.4 11.2 %copy-start.1 = (f32[3,3,64,64]{3,2,1,0:T(8,128)S(1)}, f32[3,3,64,64]{3,2,1,0:T(8,128)}, u32[]{:S(2)}) copy-start(f32[3,3,64,64]{3,2,1,0:T(8,128)} %weight_ref.6) | copy-start | bytes 442372

commit v4 on v3

--- a/solution.py
+++ b/solution.py
@@ -248,9 +248,9 @@
     return jnp.concatenate([row, row], axis=1)
 
 
-def exact_dot(left, right, dims):
+def close_dot(left, right, dims):
     return lax.dot_general(
-        left, right, (dims, ((), ())), precision=highest, preferred_element_type=jnp.float32
+        left, right, (dims, ((), ())), precision=lax.Precision.HIGH, preferred_element_type=jnp.float32
     )
 
 
@@ -369,7 +369,7 @@
 
 
 def kernel_rows(joined, grad):
-    return tap_rows(exact_dot(joined, spread_shifts(grad), ((0,), (0,))))
+    return tap_rows(close_dot(joined, spread_shifts(grad), ((0,), (0,))))
 
 
 def kernel_rows_and_sums(joined, grad, devices):
@@ -378,7 +378,7 @@
     step = 4 * SLOTS
     outside = ((tap == 0) & (row >= ROWS - step)) | ((tap == 2) & (row < step))
     ones = jnp.where(outside, 0.0, 1.0)
-    product = exact_dot(
+    product = close_dot(
         joined, jnp.concatenate([spread_shifts(grad), ones], axis=1), ((0,), (0,))
     )
     part = product[:, 3 * LANES :]
@@ -396,7 +396,7 @@
     owner = lax.broadcasted_iota(jnp.int32, (devices, total), 0)
     index = lax.broadcasted_iota(jnp.int32, (devices, total), 1)
     picked = (index // share == owner).astype(jnp.float32)
-    return tap_rows(product), exact_dot(picked, sums, ((1,), (0,)))
+    return tap_rows(product), close_dot(picked, sums, ((1,), (0,)))
 
 
 def widen_sums(row, share):
@@ -485,7 +485,7 @@
 def conv_one_kernel(devices, x_ref, weight_ref, g_ref, hidden_ref, send_ref):
     stride = SLOTS + 1
     hidden = shifted_sum(
-        exact_dot(neighbours(x_ref[...]), forward_weight(weight_ref), ((1,), (0,)))
+        close_dot(neighbours(x_ref[...]), forward_weight(weight_ref), ((1,), (0,)))
     )
     hidden_ref[...] = hidden
     stats = local_stats(hidden)
@@ -505,7 +505,7 @@
     active = elu_value(normed * affine_ref[0:1, :] + affine_ref[2:3, :])
     active_ref[...] = active
     second = shifted_sum(
-        exact_dot(neighbours(active), forward_weight(weight_ref), ((1,), (0,)))
+        close_dot(neighbours(active), forward_weight(weight_ref), ((1,), (0,)))
     )
     second_ref[...] = second
     stats = local_stats(second)
@@ -559,7 +559,7 @@
         shift_sum, gain_sum, cells,
     )
     grad_active = shifted_sum(
-        exact_dot(neighbours(grad_second), backward_weight(weight_ref), ((1,), (1,)))
+        close_dot(neighbours(grad_second), backward_weight(weight_ref), ((1,), (1,)))
     )
     normed = normed_ref[...]
     before = normed * affine_ref[0:1, :] + affine_ref[2:3, :]
@@ -583,6 +583,10 @@
     return total
 
 
+def owner_core(device):
+    return device // 4 % 2
+
+
 def back_one_kernel(
     devices, share, residues, recv_ref, before_ref, normed_ref, inverse_ref, sum_ref, weight_ref,
     affine_ref, normed_recv_ref, total_ref, send_ref,
@@ -596,7 +600,7 @@
         before_ref[...], normed_ref[...], inverse, gain, shift_sum, gain_sum, cells
     )
     field = sum_ref[...] + shifted_sum(
-        exact_dot(neighbours(grad_first), backward_weight(weight_ref), ((1,), (1,)))
+        close_dot(neighbours(grad_first), backward_weight(weight_ref), ((1,), (1,)))
     )
     one = reduce_share(recv_ref, devices, 0, share, stride)
     two = reduce_share(recv_ref, devices, share, share, stride)
@@ -606,43 +610,51 @@
         one - constant * (shift_sum / cells) - rows[:share] * (gain_sum / cells)
     )
     one, two = one / residues, two / residues
-    stride = 2 * share + SLOTS
+    stride = share + SLOTS
     for d in range(devices):
         begin = d * stride
         send_ref[begin : begin + SLOTS, :] = field[d * SLOTS : (d + 1) * SLOTS]
-        send_ref[begin + SLOTS : begin + SLOTS + share, :] = one
-        send_ref[begin + SLOTS + share : begin + stride, :] = two
-
-
-def last_kernel(
+        send_ref[begin + SLOTS : begin + stride, :] = two if owner_core(d) else one
+
+
+def map_kernel(
     table, share, residues, sym_recv_ref, recv_ref, total_one_ref, total_two_ref,
-    sym_ref, map_ref, one_ref, two_ref, gain_ref, shift_ref, scratch_ref, rows_ref,
+    sym_ref, map_ref, gain_ref, shift_ref, scratch_ref, other_ref,
 ):
-    stride = 2 * share + SLOTS
     unpack_rows(table, sym_recv_ref, scratch_ref, SLOTS + 1, 0)
     join_phases(scratch_ref, sym_ref)
-    unpack_rows(table, recv_ref, scratch_ref, stride, 0)
-    join_phases(scratch_ref, map_ref)
-    for index, out_ref in ((0, one_ref), (1, two_ref)):
-        for d in range(len(table)):
-            begin = d * stride + SLOTS + index * share
-            rows_ref[d * share : (d + 1) * share, :] = recv_ref[begin : begin + share, :]
-        for tap in range(9):
-            block = rows_ref[tap * HALF // 2 : (tap + 1) * HALF // 2, :]
-            out_ref[tap, : HALF // 2, :] = block[:, :HALF]
-            out_ref[tap, HALF // 2 :, :] = swap_halves(block)[:, :HALF]
+    unpack_rows(table, recv_ref, other_ref, share + SLOTS, 0)
+    join_phases(other_ref, map_ref)
     for index, total_ref in ((0, total_one_ref), (1, total_two_ref)):
         total = total_ref[...] / residues
         shift_ref[index : index + 1, :] = total[:, :HALF]
         gain_ref[index : index + 1, :] = swap_halves(total)[:, :HALF]
 
 
-def call(body, shapes, scratch=()):
+def grad_kernel(devices, share, mine_ref, partner_ref, one_ref, two_ref, first_ref, second_ref):
+    stride = share + SLOTS
+    for source_ref, rows_ref in ((mine_ref, first_ref), (partner_ref, second_ref)):
+        for d in range(devices):
+            begin = d * stride + SLOTS
+            rows_ref[d * share : (d + 1) * share, :] = source_ref[begin : begin + share, :]
+    even = lax.axis_index("row") % 2 == 0
+    for tap in range(9):
+        begin = tap * HALF // 2
+        mine = first_ref[begin : begin + HALF // 2, :]
+        partner = second_ref[begin : begin + HALF // 2, :]
+        one, two = jnp.where(even, mine, partner), jnp.where(even, partner, mine)
+        for block, out_ref in ((one, one_ref), (two, two_ref)):
+            out_ref[tap, : HALF // 2, :] = block[:, :HALF]
+            out_ref[tap, HALF // 2 :, :] = swap_halves(block)[:, :HALF]
+
+
+def call(body, shapes, scratch=(), cost=None):
     return pl.pallas_call(
         body,
         out_shape=[jax.ShapeDtypeStruct(s, jnp.float32) for s in shapes],
         scratch_shapes=[pltpu.VMEM(s, jnp.float32) for s in scratch],
         compiler_params=pltpu.CompilerParams(vmem_limit_bytes=VMEM_BYTES),
+        cost_estimate=cost,
     )
 
 
@@ -687,18 +699,21 @@
     )
     recv = exchange(send, devices)
     total_one, send = call(
-        part(back_one_kernel, devices, share, residues), [line, wide(2 * share + SLOTS)]
+        part(back_one_kernel, devices, share, residues), [line, wide(share + SLOTS)]
     )(recv, grad_before, normed_one, inverse_one, grad_sum, conv_one, affine, normed_recv)
     recv = exchange(send, devices)
     taps = conv_one.shape[0] * conv_one.shape[1]
-    sym_out, grad_map, grad_one, grad_two, grad_gain, grad_shift = call(
-        part(last_kernel, table, share, residues),
-        [
-            pair_map.shape, pair_map.shape, (taps, HALF, HALF), (taps, HALF, HALF),
-            norm_gain.shape, norm_shift.shape,
-        ],
-        [whole, rows],
+    cores = [(i, i ^ 1) for i in range(lax.axis_size("row"))]
+    partner = lax.ppermute(recv, "row", cores)
+    sym_out, grad_map, grad_gain, grad_shift = call(
+        part(map_kernel, table, share, residues),
+        [pair_map.shape, pair_map.shape, norm_gain.shape, norm_shift.shape],
+        [whole, whole],
+        pl.CostEstimate(flops=4 << 20, bytes_accessed=4 << 20, transcendentals=0),
     )(sym_recv, recv, total_one, total_two)
+    grad_one, grad_two = call(
+        part(grad_kernel, devices, share), [(taps, HALF, HALF)] * 2, [rows, rows]
+    )(recv, partner)
     return (
         sym_out,
         grad_map,

time: 84 us -> 81.2 us (0.967)
  blocking collectives: 74.8 us -> 72.9 us
    all_to_all x6, blocking collectives: 74.8 us -> 72.9 us  [exchange(): lax.all_to_all(sent, AXES, split_axis=0, concat_axis=0, tiled=True)]
    pallas_call x2 -> x3, Pallas kernels: 1.87 us -> 2.39 us  [the longest x1 1 us: phase_body(): call(part(grad_kernel, devices, share), [(taps, HALF, HALF)] * 2, [rows,...]
  transfers between devices with their start and end apart: 0 -> 1, of which waited for: 0 -> 1; matrix products, arithmetic and copies ran while one was open for 0% -> 0% of each run, Pallas kernels for 0% -> 1%
where the time goes in v4:
time: 81.2 us; the launch traced here: 80.9 us
  blocking collectives  72.9 us (90%)
  Pallas kernels  6.54 us (8%)
    all_to_all x6, blocking collectives, exchange(): lax.all_to_all(sent, AXES, split_axis=0, concat_axis=0, tiled=True)  72.9 us
  transfers between devices with their start and end apart: 1, of which 1 were waited for; matrix products, arithmetic and copies ran while one was open for 0% of the time, Pallas kernels for 1%

profile of v4, /device:TPU:0, one launch (start us, length us, event | category | flops | bytes accessed | tf_op | source)
XLA Modules:
  0.0 80.9 jit_solution(17270552307074482715)
XLA Ops:
  0.6 0.0 copy-start
  0.6 1.2 %shard_map.109 = (f32[256,128]{1,0:T(8,128)S(1)}, f32[256,128]{1,0:T(8,128)S(1)}, f32[8,128]{1,0:T(8,128)S(1)}) custom-call(f32[16,2048]{1,0:T(8,128)} %x_ref.1, f32[16,2048]{1,0:T(8,128)} %g_ref.1, f32[2,64]{1,0:T(2,128)} %gain_ref.1, f32[2,64]{1,0:T(2,128)} %shift_ref.1), custom_call_target="tpu_custom_call" | custom-call | tf_op jit(solution)/shard_map/pallas_call | solution.py:679
  1.9 15.5 %all_to_all.30 = f32[32,1,1024]{2,1,0:T(1,128)S(1)} all-to-all(f32[32,1,1024]{2,1,0:T(1,128)S(1)} %bitcast.33), channel_id=1, replica_groups=mesh['row'=8,'col'=4] {'row','col'}, dimensions={0} | all-to-all | bytes 262144 | tf_op jit(solution)/shard_map/all_to_all | solution.py:663
  17.4 0.0 copy-done
  17.4 0.0 copy-start.1
  17.4 0.7 shard_map.110
  18.1 10.3 %all_to_all.31 = f32[32,1,1152]{2,1,0:T(1,128)S(1)} all-to-all(f32[32,1,1152]{2,1,0:T(1,128)S(1)} %bitcast.32), channel_id=1, replica_groups=mesh['row'=8,'col'=4] {'row','col'}, dimensions={0} | all-to-all | bytes 294912 | tf_op jit(solution)/shard_map/all_to_all | solution.py:663
  28.4 0.0 copy-done.1
  28.4 0.9 %shard_map.111 = (f32[256,128]{1,0:T(8,128)S(1)}, f32[1,128]{1,0:T(1,128)S(1)}, f32[256,128]{1,0:T(8,128)S(1)}, f32[256,128]{1,0:T(8,128)S(1)}, f32[352,128]{1,0:T(8,128)S(1)}) custom-call(f32[288,128]{1,0:T(8,128)S(1)} %bitcast.25, f32[256,128]{1,0:T(8,128)S(1)} %get-tuple-element.34.hidden_ref, f32[256,128]{1,0:T(8,128)S(1)} %bitcast.15, ...), custom_call_target="tpu_custom_call" | custom-call | tf_op jit(solution)/shard_map/pallas_call | solution.py:687
  29.3 10.8 %all_to_all.32 = f32[32,1,1408]{2,1,0:T(1,128)S(1)} all-to-all(f32[32,1,1408]{2,1,0:T(1,128)S(1)} %bitcast.30), channel_id=1, replica_groups=mesh['row'=8,'col'=4] {'row','col'}, dimensions={0} | all-to-all | bytes 360448 | tf_op jit(solution)/shard_map/all_to_all | solution.py:663
  40.1 0.3 shard_map.112
  40.4 10.5 %all_to_all.33 = f32[32,1,1152]{2,1,0:T(1,128)S(1)} all-to-all(f32[32,1,1152]{2,1,0:T(1,128)S(1)} %bitcast.31), channel_id=1, replica_groups=mesh['row'=8,'col'=4] {'row','col'}, dimensions={0} | all-to-all | bytes 294912 | tf_op jit(solution)/shard_map/all_to_all | solution.py:663
  50.8 1.1 %shard_map.113 = (f32[256,128]{1,0:T(8,128)S(1)}, f32[1,128]{1,0:T(1,128)S(1)}, f32[608,128]{1,0:T(8,128)S(1)}) custom-call(f32[288,128]{1,0:T(8,128)S(1)} %bitcast.23, f32[256,128]{1,0:T(8,128)S(1)} %get-tuple-element.39.sum_ref, f32[256,128]{1,0:T(8,128)S(1)} %get-tuple-element.40.normed_two_ref, f32[1,128]{1,0:T(1,128)S(1)} %get-tuple-element.41.inverse_two_ref, ...), custom_call_target="tpu_custom_call" | custom-call | tf_op jit(solution)/shard_map/pallas_call | solution.py:695
  51.9 12.6 %all_to_all.34 = f32[32,1,2432]{2,1,0:T(1,128)S(1)} all-to-all(f32[32,1,2432]{2,1,0:T(1,128)S(1)} %bitcast.28), channel_id=1, replica_groups=mesh['row'=8,'col'=4] {'row','col'}, dimensions={0} | all-to-all | bytes 622592 | tf_op jit(solution)/shard_map/all_to_all | solution.py:663
  64.5 0.5 shard_map.114
  65.0 13.3 %all_to_all.35 = f32[32,1,2176]{2,1,0:T(1,128)S(1)} all-to-all(f32[32,1,2176]{2,1,0:T(1,128)S(1)} %bitcast.29), channel_id=1, replica_groups=mesh['row'=8,'col'=4] {'row','col'}, dimensions={0} | all-to-all | bytes 557056 | tf_op jit(solution)/shard_map/all_to_all | solution.py:663
  78.3 0.4 collective-permute-start
  78.7 0.9 %shard_map.115 = (f32[16,2048]{1,0:T(8,128)}, f32[16,2048]{1,0:T(8,128)}, f32[2,64]{1,0:T(2,128)}, f32[2,64]{1,0:T(2,128)}) custom-call(f32[288,128]{1,0:T(8,128)S(1)} %bitcast.24, f32[544,128]{1,0:T(8,128)S(1)} %bitcast.19, f32[1,128]{1,0:T(1,128)S(1)} %get-tuple-element.48.total_one_ref, f32[1,128]{1,0:T(1,128)S(1)} %get-tuple-element.49.total_two_ref), custom_call_target="tpu_custom_call" | custom-call | flops 4194304 | bytes 4194304 | tf_op jit(solution)/shard_map/pallas_call | solution.py:708
  79.6 0.3 collective-permute-done.partner_ref
  79.9 1.0 %shard_map.116 = (f32[9,64,64]{2,1,0:T(8,128)}, f32[9,64,64]{2,1,0:T(8,128)}) custom-call(f32[544,128]{1,0:T(8,128)S(1)} %bitcast.20, f32[544,128]{1,0:T(8,128)S(1)} %collective-permute-done.partner_ref), custom_call_target="tpu_custom_call" | custom-call | tf_op jit(solution)/shard_map/pallas_call | solution.py:714
Async XLA Ops:
  0.6 16.8 %copy-start = (f32[3,3,64,64]{3,2,1,0:T(8,128)S(1)}, f32[3,3,64,64]{3,2,1,0:T(8,128)}, u32[]{:S(2)}) copy-start(f32[3,3,64,64]{3,2,1,0:T(8,128)} %weight_ref.7) | copy-start | bytes 442372
  17.4 11.0 %copy-start.1 = (f32[3,3,64,64]{3,2,1,0:T(8,128)S(1)}, f32[3,3,64,64]{3,2,1,0:T(8,128)}, u32[]{:S(2)}) copy-start(f32[3,3,64,64]{3,2,1,0:T(8,128)} %weight_ref.6) | copy-start | bytes 442372
  78.3 1.6 %collective-permute-start = (f32[544,128]{1,0:T(8,128)S(1)}, f32[544,128]{1,0:T(8,128)S(1)}, u32[]{:S(2)}, u32[]{:S(2)}) collective-permute-start(f32[544,128]{1,0:T(8,128)S(1)} %bitcast.18), channel_id=1, source_target_pairs={{0,4},{4,0},{8,12},{12,8},{16,20},{20,16},{24,28},{28,24},{1,5},{5... | collective-permute-start | bytes 835592 | tf_op jit(solution)/shard_map/ppermute | solution.py:707

commit v5 on v4

--- a/solution.py
+++ b/solution.py
@@ -548,8 +548,8 @@
 
 
 def back_two_kernel(
-    devices, share, recv_ref, sum_ref, normed_two_ref, inverse_two_ref, active_ref, normed_ref,
-    x_ref, weight_ref, affine_ref, before_ref, total_ref, send_ref, two_ref, one_ref,
+    devices, recv_ref, sum_ref, normed_two_ref, inverse_two_ref, active_ref, normed_ref,
+    x_ref, weight_ref, affine_ref, before_ref, total_ref, sums_ref, keep_ref, give_ref,
 ):
     cells = 2.0 * ROWS * devices
     shift_sum, gain_sum = split_sums(recv_ref[pl.ds(SLOTS, devices, stride=SLOTS + 1), :])
@@ -565,21 +565,36 @@
     before = normed * affine_ref[0:1, :] + affine_ref[2:3, :]
     grad_before = grad_active * jnp.where(before > 0, 1.0, jnp.exp(jnp.minimum(before, 0.0)))
     before_ref[...] = grad_before
-    sums = pair_sums(grad_before, normed)
-    two_ref[...] = kernel_rows(neighbours(active_ref[...]), grad_second)
-    one_ref[...] = kernel_rows(neighbours(x_ref[...]), grad_before)
-    stride = 2 * share + 1
+    sums_ref[...] = pair_sums(grad_before, normed)
+    two = kernel_rows(neighbours(active_ref[...]), grad_second)
+    one = kernel_rows(neighbours(x_ref[...]), grad_before)
+    even = lax.axis_index("row") % 2 == 0
+    keep_ref[...] = jnp.where(even, one, two)
+    give_ref[...] = jnp.where(even, two, one)
+
+
+def pair_kernel(devices, share, keep_ref, got_ref, sums_ref, before_exchange_ref, send_ref):
+    del before_exchange_ref
+    stride = share + 1
+    sums = sums_ref[...]
     for d in range(devices):
-        begin = d * stride
-        send_ref[begin : begin + share, :] = one_ref[d * share : (d + 1) * share, :]
-        send_ref[begin + share : begin + 2 * share, :] = two_ref[d * share : (d + 1) * share, :]
-        send_ref[begin + 2 * share : begin + stride, :] = sums
-
-
-def reduce_share(ref, devices, begin, size, stride):
-    total = ref[begin : begin + size, :]
-    for d in range(1, devices):
-        total = total + ref[d * stride + begin : d * stride + begin + size, :]
+        rows = slice(d * share, (d + 1) * share)
+        send_ref[d * stride : d * stride + share, :] = keep_ref[rows, :] + got_ref[rows, :]
+        send_ref[d * stride + share : (d + 1) * stride, :] = sums
+
+
+def constant_kernel(devices, share, recv_ref, weight_ref, rows_ref, constant_ref, joined_ref):
+    rows = reduce_share(recv_ref, range(devices), 0, share + 1, share + 2)
+    rows_ref[...] = rows[:share]
+    constant_ref[...] = widen_sums(rows[share : share + 1], share)
+    joined_ref[...] = backward_weight(weight_ref)
+
+
+def reduce_share(ref, sources, begin, size, stride):
+    total = None
+    for d in sources:
+        rows = ref[d * stride + begin : d * stride + begin + size, :]
+        total = rows if total is None else total + rows
     return total
 
 
@@ -588,26 +603,25 @@
 
 
 def back_one_kernel(
-    devices, share, residues, recv_ref, before_ref, normed_ref, inverse_ref, sum_ref, weight_ref,
-    affine_ref, normed_recv_ref, total_ref, send_ref,
+    devices, share, residues, recv_ref, before_ref, normed_ref, inverse_ref, sum_ref, joined_ref,
+    affine_ref, rows_ref, constant_ref, total_ref, send_ref,
 ):
     cells = 2.0 * ROWS * devices
-    stride = 2 * share + 1
-    shift_sum, gain_sum = split_sums(recv_ref[pl.ds(2 * share, devices, stride=stride), :])
+    stride = share + 1
+    shift_sum, gain_sum = split_sums(recv_ref[pl.ds(share, devices, stride=stride), :])
     total_ref[...] = jnp.where(lane_low((1, LANES)), shift_sum, gain_sum)
     gain, inverse = affine_ref[0:1, :], inverse_ref[...]
     grad_first = norm_back(
         before_ref[...], normed_ref[...], inverse, gain, shift_sum, gain_sum, cells
     )
     field = sum_ref[...] + shifted_sum(
-        close_dot(neighbours(grad_first), backward_weight(weight_ref), ((1,), (1,)))
-    )
-    one = reduce_share(recv_ref, devices, 0, share, stride)
-    two = reduce_share(recv_ref, devices, share, share, stride)
-    rows = reduce_share(normed_recv_ref, devices, 0, share + 1, share + 2)
-    constant = widen_sums(rows[share : share + 1], share)
+        close_dot(neighbours(grad_first), joined_ref[...], ((1,), (1,)))
+    )
+    sources = range(devices)
+    one = reduce_share(recv_ref, [d for d in sources if not owner_core(d)], 0, share, stride)
+    two = reduce_share(recv_ref, [d for d in sources if owner_core(d)], 0, share, stride)
     one = (inverse * gain) * (
-        one - constant * (shift_sum / cells) - rows[:share] * (gain_sum / cells)
+        one - constant_ref[...] * (shift_sum / cells) - rows_ref[...] * (gain_sum / cells)
     )
     one, two = one / residues, two / residues
     stride = share + SLOTS
@@ -692,24 +706,36 @@
         part(output_kernel, devices, share), [whole, line, whole, wide(SLOTS + 1)]
     )(normed_recv, second, x, grad_recv, affine)
     sym_recv = exchange(send, devices)
-    grad_before, total_two, send = call(
-        part(back_two_kernel, devices, share), [whole, line, wide(2 * share + 1)], [rows, rows]
+    cores = [(i, i ^ 1) for i in range(lax.axis_size("row"))]
+    cost = pl.CostEstimate(flops=4 << 20, bytes_accessed=4 << 20, transcendentals=0)
+    grad_before, total_two, sums, keep, give = call(
+        part(back_two_kernel, devices), [whole, line, line, rows, rows]
     )(
         sym_recv, grad_sum, normed_two, inverse_two, active, normed_one, x, conv_two, affine
+    )
+    got = lax.ppermute(give, "row", cores)
+    normed_rows, constant, joined = call(
+        part(constant_kernel, devices, share),
+        [(share, LANES), (share, LANES), (3 * LANES, 2 * LANES)],
+        cost=cost,
+    )(normed_recv, conv_one)
+    (send,) = call(part(pair_kernel, devices, share), [wide(share + 1)])(
+        keep, got, sums, constant
     )
     recv = exchange(send, devices)
     total_one, send = call(
         part(back_one_kernel, devices, share, residues), [line, wide(share + SLOTS)]
-    )(recv, grad_before, normed_one, inverse_one, grad_sum, conv_one, affine, normed_recv)
+    )(
+        recv, grad_before, normed_one, inverse_one, grad_sum, joined, affine, normed_rows, constant
+    )
     recv = exchange(send, devices)
     taps = conv_one.shape[0] * conv_one.shape[1]
-    cores = [(i, i ^ 1) for i in range(lax.axis_size("row"))]
     partner = lax.ppermute(recv, "row", cores)
     sym_out, grad_map, grad_gain, grad_shift = call(
         part(map_kernel, table, share, residues),
         [pair_map.shape, pair_map.shape, norm_gain.shape, norm_shift.shape],
         [whole, whole],
-        pl.CostEstimate(flops=4 << 20, bytes_accessed=4 << 20, transcendentals=0),
+        cost,
     )(sym_recv, recv, total_one, total_two)
     grad_one, grad_two = call(
         part(grad_kernel, devices, share), [(taps, HALF, HALF)] * 2, [rows, rows]

time: 81.2 us -> 79.4 us (0.978)
  blocking collectives: 72.9 us -> 69.8 us
  waiting for transfers between devices: 0.29 us -> 1.47 us
    all_to_all x6, blocking collectives: 72.9 us -> 69.8 us  [exchange(): lax.all_to_all(sent, AXES, split_axis=0, concat_axis=0, tiled=True)]
    ppermute x0 -> x1, waiting for transfers between devices: none -> 1.18 us  [phase_body(): got = lax.ppermute(give, 'row', cores)]
  transfers between devices with their start and end apart: 1 -> 2, of which waited for: 1 -> 2; matrix products, arithmetic and copies ran while one was open for 0% -> 0% of each run, Pallas kernels for 1% -> 1%
where the time goes in v5:
time: 79.4 us; the launch traced here: 79.1 us
  blocking collectives  69.8 us (88%)
  Pallas kernels  6.62 us (8%)
  waiting for transfers between devices  1.47 us (2%)
    all_to_all x6, blocking collectives, exchange(): lax.all_to_all(sent, AXES, split_axis=0, concat_axis=0, tiled=True)  69.8 us
  transfers between devices with their start and end apart: 2, of which 2 were waited for; matrix products, arithmetic and copies ran while one was open for 0% of the time, Pallas kernels for 1%

profile of v5, /device:TPU:0, one launch (start us, length us, event | category | flops | bytes accessed | tf_op | source)
XLA Modules:
  0.0 79.1 jit_solution(16606816274400126173)
XLA Ops:
  0.6 0.0 copy-start
  0.6 1.2 %shard_map.109 = (f32[256,128]{1,0:T(8,128)S(1)}, f32[256,128]{1,0:T(8,128)S(1)}, f32[8,128]{1,0:T(8,128)S(1)}) custom-call(f32[16,2048]{1,0:T(8,128)} %x_ref.1, f32[16,2048]{1,0:T(8,128)} %g_ref.1, f32[2,64]{1,0:T(2,128)} %gain_ref.1, f32[2,64]{1,0:T(2,128)} %shift_ref.1), custom_call_target="tpu_custom_call" | custom-call | tf_op jit(solution)/shard_map/pallas_call | solution.py:693
  1.9 15.5 %all_to_all.30 = f32[32,1,1024]{2,1,0:T(1,128)S(1)} all-to-all(f32[32,1,1024]{2,1,0:T(1,128)S(1)} %bitcast.33), channel_id=1, replica_groups=mesh['row'=8,'col'=4] {'row','col'}, dimensions={0} | all-to-all | bytes 262144 | tf_op jit(solution)/shard_map/all_to_all | solution.py:677
  17.4 0.0 copy-done
  17.4 0.0 copy-start.1
  17.4 0.7 shard_map.110
  18.1 10.3 %all_to_all.31 = f32[32,1,1152]{2,1,0:T(1,128)S(1)} all-to-all(f32[32,1,1152]{2,1,0:T(1,128)S(1)} %bitcast.32), channel_id=1, replica_groups=mesh['row'=8,'col'=4] {'row','col'}, dimensions={0} | all-to-all | bytes 294912 | tf_op jit(solution)/shard_map/all_to_all | solution.py:677
  28.4 0.0 copy-done.1
  28.4 0.9 %shard_map.111 = (f32[256,128]{1,0:T(8,128)S(1)}, f32[1,128]{1,0:T(1,128)S(1)}, f32[256,128]{1,0:T(8,128)S(1)}, f32[256,128]{1,0:T(8,128)S(1)}, f32[352,128]{1,0:T(8,128)S(1)}) custom-call(f32[288,128]{1,0:T(8,128)S(1)} %bitcast.25, f32[256,128]{1,0:T(8,128)S(1)} %get-tuple-element.39.hidden_ref, f32[256,128]{1,0:T(8,128)S(1)} %bitcast.15, ...), custom_call_target="tpu_custom_call" | custom-call | tf_op jit(solution)/shard_map/pallas_call | solution.py:701
  29.3 10.8 %all_to_all.32 = f32[32,1,1408]{2,1,0:T(1,128)S(1)} all-to-all(f32[32,1,1408]{2,1,0:T(1,128)S(1)} %bitcast.30), channel_id=1, replica_groups=mesh['row'=8,'col'=4] {'row','col'}, dimensions={0} | all-to-all | bytes 360448 | tf_op jit(solution)/shard_map/all_to_all | solution.py:677
  40.1 0.3 shard_map.112
  40.4 10.5 %all_to_all.33 = f32[32,1,1152]{2,1,0:T(1,128)S(1)} all-to-all(f32[32,1,1152]{2,1,0:T(1,128)S(1)} %bitcast.31), channel_id=1, replica_groups=mesh['row'=8,'col'=4] {'row','col'}, dimensions={0} | all-to-all | bytes 294912 | tf_op jit(solution)/shard_map/all_to_all | solution.py:677
  50.8 1.0 %shard_map.113 = (f32[256,128]{1,0:T(8,128)S(1)}, f32[1,128]{1,0:T(1,128)S(1)}, f32[1,128]{1,0:T(1,128)S(1)}, f32[288,128]{1,0:T(8,128)S(1)}, f32[288,128]{1,0:T(8,128)S(1)}) custom-call(f32[288,128]{1,0:T(8,128)S(1)} %bitcast.23, f32[256,128]{1,0:T(8,128)S(1)} %get-tuple-element.44.sum_ref, f32[256,128]{1,0:T(8,128)S(1)} %get-tuple-element.45.normed_two_ref, ...), custom_call_target="tpu_custom_call" | custom-call | tf_op jit(solution)/shard_map/pallas_call | solution.py:711
  51.9 0.1 collective-permute-start
  51.9 0.2 shard_map.114
  52.1 1.2 %collective-permute-done.got_ref = f32[288,128]{1,0:T(8,128)S(1)} collective-permute-done((f32[288,128]{1,0:T(8,128)S(1)}, f32[288,128]{1,0:T(8,128)S(1)}, u32[]{:S(2)}, u32[]{:S(2)}) %collective-permute-start) | collective-permute-done | bytes 147488 | tf_op jit(solution)/shard_map/ppermute | solution.py:716
  53.3 10.6 %all_to_all.34 = f32[32,1,1280]{2,1,0:T(1,128)S(1)} all-to-all(f32[32,1,1280]{2,1,0:T(1,128)S(1)} %bitcast.28), channel_id=1, replica_groups=mesh['row'=8,'col'=4] {'row','col'}, dimensions={0} | all-to-all | bytes 327680 | tf_op jit(solution)/shard_map/all_to_all | solution.py:677
  63.9 0.4 shard_map.116
  64.3 12.2 %all_to_all.35 = f32[32,1,2176]{2,1,0:T(1,128)S(1)} all-to-all(f32[32,1,2176]{2,1,0:T(1,128)S(1)} %bitcast.29), channel_id=1, replica_groups=mesh['row'=8,'col'=4] {'row','col'}, dimensions={0} | all-to-all | bytes 557056 | tf_op jit(solution)/shard_map/all_to_all | solution.py:677
  76.5 0.4 collective-permute-start.1
  77.0 0.9 %shard_map.117 = (f32[16,2048]{1,0:T(8,128)}, f32[16,2048]{1,0:T(8,128)}, f32[2,64]{1,0:T(2,128)}, f32[2,64]{1,0:T(2,128)}) custom-call(f32[288,128]{1,0:T(8,128)S(1)} %bitcast.24, f32[544,128]{1,0:T(8,128)S(1)} %bitcast.19, f32[1,128]{1,0:T(1,128)S(1)} %get-tuple-element.58.total_one_ref, f32[1,128]{1,0:T(1,128)S(1)} %get-tuple-element.59.total_two_ref), custom_call_target="tpu_custom_call" | custom-call | flops 4194304 | bytes 4194304 | tf_op jit(solution)/shard_map/pallas_call | solution.py:734
  77.9 0.3 collective-permute-done.1.partner_ref
  78.1 1.0 %shard_map.118 = (f32[9,64,64]{2,1,0:T(8,128)}, f32[9,64,64]{2,1,0:T(8,128)}) custom-call(f32[544,128]{1,0:T(8,128)S(1)} %bitcast.20, f32[544,128]{1,0:T(8,128)S(1)} %collective-permute-done.1.partner_ref), custom_call_target="tpu_custom_call" | custom-call | tf_op jit(solution)/shard_map/pallas_call | solution.py:740
  (1 shorter events, 0.0 us)
Async XLA Ops:
  0.6 16.8 %copy-start = (f32[3,3,64,64]{3,2,1,0:T(8,128)S(1)}, f32[3,3,64,64]{3,2,1,0:T(8,128)}, u32[]{:S(2)}) copy-start(f32[3,3,64,64]{3,2,1,0:T(8,128)} %weight_ref.7) | copy-start | bytes 442372
  17.4 11.0 %copy-start.1 = (f32[3,3,64,64]{3,2,1,0:T(8,128)S(1)}, f32[3,3,64,64]{3,2,1,0:T(8,128)}, u32[]{:S(2)}) copy-start(f32[3,3,64,64]{3,2,1,0:T(8,128)} %weight_ref.6) | copy-start | bytes 442372
  51.9 1.4 %collective-permute-start = (f32[288,128]{1,0:T(8,128)S(1)}, f32[288,128]{1,0:T(8,128)S(1)}, u32[]{:S(2)}, u32[]{:S(2)}) collective-permute-start(f32[288,128]{1,0:T(8,128)S(1)} %get-tuple-element.50), channel_id=1, source_target_pairs={{0,4},{4,0},{8,12},{12,8},{16,20},{20,16},{24,28},{28,24},{1,5},{5... | collective-permute-start | bytes 442376 | tf_op jit(solution)/shard_map/ppermute | solution.py:716
  76.5 1.6 %collective-permute-start.1 = (f32[544,128]{1,0:T(8,128)S(1)}, f32[544,128]{1,0:T(8,128)S(1)}, u32[]{:S(2)}, u32[]{:S(2)}) collective-permute-start(f32[544,128]{1,0:T(8,128)S(1)} %bitcast.18), channel_id=1, source_target_pairs={{0,4},{4,0},{8,12},{12,8},{16,20},{20,16},{24,28},{28,24},{1,5},{5... | collective-permute-start | bytes 835592 | tf_op jit(solution)/shard_map/ppermute | solution.py:733

commit v6 on v5

--- a/solution.py
+++ b/solution.py
@@ -232,6 +232,10 @@
     return table
 
 
+def device_index():
+    return lax.axis_index("row") * lax.axis_size("col") + lax.axis_index("col")
+
+
 def lane_low(shape):
     return lax.broadcasted_iota(jnp.int32, shape, len(shape) - 1) < HALF
 
@@ -248,9 +252,21 @@
     return jnp.concatenate([row, row], axis=1)
 
 
+def two_parts(values):
+    high = values.astype(jnp.bfloat16)
+    return high, (values - high.astype(jnp.float32)).astype(jnp.bfloat16)
+
+
 def close_dot(left, right, dims):
+    if dims[0] == (0,):
+        left, dims = left.T, ((1,), dims[1])
+    left_high, left_low = two_parts(left)
+    right_high, right_low = two_parts(right)
     return lax.dot_general(
-        left, right, (dims, ((), ())), precision=lax.Precision.HIGH, preferred_element_type=jnp.float32
+        jnp.concatenate([left_high, left_high, left_low], axis=1),
+        jnp.concatenate([right_high, right_low, right_high], axis=dims[1][0]),
+        (dims, ((), ())),
+        preferred_element_type=jnp.float32,
     )
 
 
@@ -303,7 +319,7 @@
     zero = jnp.zeros((SLOTS, LANES), jnp.float32)
     ahead = jnp.concatenate([values[SLOTS:], zero], axis=0)
     behind = jnp.concatenate([zero, values[:-SLOTS]], axis=0)
-    place = (lax.broadcasted_iota(jnp.int32, (ROWS, LANES), 0) // SLOTS) % 4
+    place = (lax.broadcasted_iota(jnp.int32, (ROWS, LANES), 0) >> 3) & 3
     low = lane_low((ROWS, LANES))
     side = jnp.where(low, jnp.where(place == 3, 0.0, ahead), jnp.where(place == 0, 0.0, behind))
     return jnp.concatenate([side, values], axis=1)
@@ -356,15 +372,17 @@
 
 
 def tap_rows(product):
-    low = lane_low((HALF // 2, LANES))
+    quarter = HALF // 2
+    low = lane_low((quarter, LANES))
     pieces = []
     for a in range(3):
         part = product[:, a * LANES : (a + 1) * LANES]
         for even, odd in TAP_SOURCES:
-            tap = part[even * HALF : (even + 1) * HALF] + swap_halves(
-                part[odd * HALF : (odd + 1) * HALF]
-            )
-            pieces.append(jnp.where(low, tap[: HALF // 2], swap_halves(tap[HALF // 2 :])))
+            first = part[even * HALF : (even + 1) * HALF]
+            second = part[odd * HALF : (odd + 1) * HALF]
+            kept = jnp.where(low, first[:quarter], second[quarter:])
+            moved = jnp.where(low, first[quarter:], second[:quarter])
+            pieces.append(kept + swap_halves(moved))
     return jnp.concatenate(pieces, axis=0)
 
 
@@ -374,7 +392,7 @@
 
 def kernel_rows_and_sums(joined, grad, devices):
     row = lax.broadcasted_iota(jnp.int32, (ROWS, LANES), 0)
-    tap = (lax.broadcasted_iota(jnp.int32, (ROWS, LANES), 1) % HALF) % 3
+    tap = (lax.broadcasted_iota(jnp.int32, (ROWS, LANES), 1) & (HALF - 1)) >> 4
     step = 4 * SLOTS
     outside = ((tap == 0) & (row >= ROWS - step)) | ((tap == 2) & (row < step))
     ones = jnp.where(outside, 0.0, 1.0)
@@ -382,27 +400,29 @@
         joined, jnp.concatenate([spread_shifts(grad), ones], axis=1), ((0,), (0,))
     )
     part = product[:, 3 * LANES :]
-    low = lane_low((HALF // 2, LANES))
+    quarter = HALF // 2
+    low = lane_low((quarter, LANES))
+    row = lax.broadcasted_iota(jnp.int32, (quarter, LANES), 0) & 15
+    lane = lax.broadcasted_iota(jnp.int32, (quarter, LANES), 1) & (HALF - 1)
     pieces = []
     for even, odd in TAP_SOURCES:
         both = part[even * HALF : (even + 1) * HALF] + part[odd * HALF : (odd + 1) * HALF]
-        pieces.append(jnp.where(low, both[: HALF // 2], both[HALF // 2 :]))
-    sums = jnp.concatenate(pieces * 3, axis=0)
+        pieces.append(jnp.where(low, both[:quarter], both[quarter:]))
+    sums = jnp.concatenate(
+        [jnp.where(lane - 16 * a == row, piece, 0.0) for a in range(3) for piece in pieces], axis=0
+    )
     total = sums.shape[0]
     share = total // devices
-    row = lax.broadcasted_iota(jnp.int32, (total, LANES), 0)
-    lane = lax.broadcasted_iota(jnp.int32, (total, LANES), 1) % HALF
-    sums = jnp.where(lane == 3 * (row % share) + row // (total // 3), sums, 0.0)
-    owner = lax.broadcasted_iota(jnp.int32, (devices, total), 0)
+    first = share * lax.broadcasted_iota(jnp.int32, (devices, total), 0)
     index = lax.broadcasted_iota(jnp.int32, (devices, total), 1)
-    picked = (index // share == owner).astype(jnp.float32)
+    picked = jnp.where((index >= first) & (index < first + share), 1.0, 0.0)
     return tap_rows(product), close_dot(picked, sums, ((1,), (0,)))
 
 
 def widen_sums(row, share):
     lane = lax.broadcasted_iota(jnp.int32, (share, LANES), 1)
-    index = lax.broadcasted_iota(jnp.int32, (share, LANES), 0)
-    picked = jnp.where((lane % HALF) // 3 == index, row, 0.0)
+    index = lax.broadcasted_iota(jnp.int32, (share, LANES), 0) + share * device_index()
+    picked = jnp.where(lane & 15 == index & 15, row, 0.0)
     low = lane < HALF
     first = jnp.sum(jnp.where(low, picked, 0.0), axis=1, keepdims=True)
     second = jnp.sum(jnp.where(low, 0.0, picked), axis=1, keepdims=True)
@@ -465,9 +485,9 @@
 
 
 def own_mirrors():
-    me = lax.axis_index("row") * lax.axis_size("col") + lax.axis_index("col")
+    me = device_index()
     slot = lax.broadcasted_iota(jnp.int32, (SLOTS, LANES), 0)
-    return (slot % 4 == 3) & (me < DILATION_STEP // 2)
+    return (slot & 3 == 3) & (me < DILATION_STEP // 2)
 
 
 def first_kernel(
@@ -549,7 +569,7 @@
 
 def back_two_kernel(
     devices, recv_ref, sum_ref, normed_two_ref, inverse_two_ref, active_ref, normed_ref,
-    x_ref, weight_ref, affine_ref, before_ref, total_ref, sums_ref, keep_ref, give_ref,
+    x_ref, weight_ref, affine_ref, before_ref, total_ref, sums_ref, second_ref, give_ref,
 ):
     cells = 2.0 * ROWS * devices
     shift_sum, gain_sum = split_sums(recv_ref[pl.ds(SLOTS, devices, stride=SLOTS + 1), :])
@@ -566,15 +586,19 @@
     grad_before = grad_active * jnp.where(before > 0, 1.0, jnp.exp(jnp.minimum(before, 0.0)))
     before_ref[...] = grad_before
     sums_ref[...] = pair_sums(grad_before, normed)
-    two = kernel_rows(neighbours(active_ref[...]), grad_second)
-    one = kernel_rows(neighbours(x_ref[...]), grad_before)
-    even = lax.axis_index("row") % 2 == 0
-    keep_ref[...] = jnp.where(even, one, two)
-    give_ref[...] = jnp.where(even, two, one)
-
-
-def pair_kernel(devices, share, keep_ref, got_ref, sums_ref, before_exchange_ref, send_ref):
-    del before_exchange_ref
+    second_ref[...] = grad_second
+    even = first_core()
+    give_ref[...] = kernel_rows(
+        neighbours(jnp.where(even, active_ref[...], x_ref[...])),
+        jnp.where(even, grad_second, grad_before),
+    )
+
+
+def first_core():
+    return lax.axis_index("row") & 1 == 0
+
+
+def pair_kernel(devices, share, keep_ref, got_ref, sums_ref, send_ref):
     stride = share + 1
     sums = sums_ref[...]
     for d in range(devices):
@@ -583,7 +607,15 @@
         send_ref[d * stride + share : (d + 1) * stride, :] = sums
 
 
-def constant_kernel(devices, share, recv_ref, weight_ref, rows_ref, constant_ref, joined_ref):
+def keep_kernel(
+    devices, share, recv_ref, weight_ref, before_ref, x_ref, second_ref, active_ref,
+    keep_ref, rows_ref, constant_ref, joined_ref,
+):
+    even = first_core()
+    keep_ref[...] = kernel_rows(
+        neighbours(jnp.where(even, x_ref[...], active_ref[...])),
+        jnp.where(even, before_ref[...], second_ref[...]),
+    )
     rows = reduce_share(recv_ref, range(devices), 0, share + 1, share + 2)
     rows_ref[...] = rows[:share]
     constant_ref[...] = widen_sums(rows[share : share + 1], share)
@@ -651,7 +683,7 @@
         for d in range(devices):
             begin = d * stride + SLOTS
             rows_ref[d * share : (d + 1) * share, :] = source_ref[begin : begin + share, :]
-    even = lax.axis_index("row") % 2 == 0
+    even = first_core()
     for tap in range(9):
         begin = tap * HALF // 2
         mine = first_ref[begin : begin + HALF // 2, :]
@@ -708,19 +740,19 @@
     sym_recv = exchange(send, devices)
     cores = [(i, i ^ 1) for i in range(lax.axis_size("row"))]
     cost = pl.CostEstimate(flops=4 << 20, bytes_accessed=4 << 20, transcendentals=0)
-    grad_before, total_two, sums, keep, give = call(
-        part(back_two_kernel, devices), [whole, line, line, rows, rows]
+    grad_before, total_two, sums, grad_second, give = call(
+        part(back_two_kernel, devices), [whole, line, line, whole, rows]
     )(
         sym_recv, grad_sum, normed_two, inverse_two, active, normed_one, x, conv_two, affine
     )
     got = lax.ppermute(give, "row", cores)
-    normed_rows, constant, joined = call(
-        part(constant_kernel, devices, share),
-        [(share, LANES), (share, LANES), (3 * LANES, 2 * LANES)],
+    keep, normed_rows, constant, joined = call(
+        part(keep_kernel, devices, share),
+        [rows, (share, LANES), (share, LANES), (3 * LANES, 2 * LANES)],
         cost=cost,
-    )(normed_recv, conv_one)
+    )(normed_recv, conv_one, grad_before, x, grad_second, active)
     (send,) = call(part(pair_kernel, devices, share), [wide(share + 1)])(
-        keep, got, sums, constant
+        keep, got, sums
     )
     recv = exchange(send, devices)
     total_one, send = call(

time: 79.4 us -> 79.3 us (level)
  transfers between devices with their start and end apart: 2 -> 2, of which waited for: 2 -> 2; matrix products, arithmetic and copies ran while one was open for 0% -> 0% of each run, Pallas kernels for 1% -> 2%
where the time goes in v6:
time: 79.3 us; the launch traced here: 79.1 us
  blocking collectives  69.8 us (88%)
  Pallas kernels  6.91 us (9%)
  waiting for transfers between devices  1.11 us (1%)
    all_to_all x6, blocking collectives, exchange(): lax.all_to_all(sent, AXES, split_axis=0, concat_axis=0, tiled=True)  69.8 us
  transfers between devices with their start and end apart: 2, of which 2 were waited for; matrix products, arithmetic and copies ran while one was open for 0% of the time, Pallas kernels for 2%

profile of v6, /device:TPU:0, one launch (start us, length us, event | category | flops | bytes accessed | tf_op | source)
XLA Modules:
  0.0 79.1 jit_solution(16001780010004959675)
XLA Ops:
  0.6 0.0 copy-start
  0.6 1.2 %shard_map.109 = (f32[256,128]{1,0:T(8,128)S(1)}, f32[256,128]{1,0:T(8,128)S(1)}, f32[8,128]{1,0:T(8,128)S(1)}) custom-call(f32[16,2048]{1,0:T(8,128)} %x_ref.1, f32[16,2048]{1,0:T(8,128)} %g_ref.1, f32[2,64]{1,0:T(2,128)} %gain_ref.1, f32[2,64]{1,0:T(2,128)} %shift_ref.1), custom_call_target="tpu_custom_call" | custom-call | tf_op jit(solution)/shard_map/pallas_call | solution.py:725
  1.9 15.5 %all_to_all.30 = f32[32,1,1024]{2,1,0:T(1,128)S(1)} all-to-all(f32[32,1,1024]{2,1,0:T(1,128)S(1)} %bitcast.34), channel_id=1, replica_groups=mesh['row'=8,'col'=4] {'row','col'}, dimensions={0} | all-to-all | bytes 262144 | tf_op jit(solution)/shard_map/all_to_all | solution.py:709
  17.4 0.0 copy-done
  17.4 0.0 copy-start.1
  17.4 0.7 shard_map.110
  18.1 10.3 %all_to_all.31 = f32[32,1,1152]{2,1,0:T(1,128)S(1)} all-to-all(f32[32,1,1152]{2,1,0:T(1,128)S(1)} %bitcast.33), channel_id=1, replica_groups=mesh['row'=8,'col'=4] {'row','col'}, dimensions={0} | all-to-all | bytes 294912 | tf_op jit(solution)/shard_map/all_to_all | solution.py:709
  28.4 0.0 copy-done.1
  28.4 0.9 %shard_map.111 = (f32[256,128]{1,0:T(8,128)S(1)}, f32[1,128]{1,0:T(1,128)S(1)}, f32[256,128]{1,0:T(8,128)S(1)}, f32[256,128]{1,0:T(8,128)S(1)}, f32[352,128]{1,0:T(8,128)S(1)}) custom-call(f32[288,128]{1,0:T(8,128)S(1)} %bitcast.26, f32[256,128]{1,0:T(8,128)S(1)} %get-tuple-element.40.hidden_ref, f32[256,128]{1,0:T(8,128)S(1)} %bitcast.15, ...), custom_call_target="tpu_custom_call" | custom-call | tf_op jit(solution)/shard_map/pallas_call | solution.py:733
  29.3 10.8 %all_to_all.32 = f32[32,1,1408]{2,1,0:T(1,128)S(1)} all-to-all(f32[32,1,1408]{2,1,0:T(1,128)S(1)} %bitcast.31), channel_id=1, replica_groups=mesh['row'=8,'col'=4] {'row','col'}, dimensions={0} | all-to-all | bytes 360448 | tf_op jit(solution)/shard_map/all_to_all | solution.py:709
  40.0 0.3 shard_map.112
  40.3 10.5 %all_to_all.33 = f32[32,1,1152]{2,1,0:T(1,128)S(1)} all-to-all(f32[32,1,1152]{2,1,0:T(1,128)S(1)} %bitcast.32), channel_id=1, replica_groups=mesh['row'=8,'col'=4] {'row','col'}, dimensions={0} | all-to-all | bytes 294912 | tf_op jit(solution)/shard_map/all_to_all | solution.py:709
  50.8 1.0 %shard_map.113 = (f32[256,128]{1,0:T(8,128)S(1)}, f32[1,128]{1,0:T(1,128)S(1)}, f32[1,128]{1,0:T(1,128)S(1)}, f32[256,128]{1,0:T(8,128)S(1)}, f32[288,128]{1,0:T(8,128)S(1)}) custom-call(f32[288,128]{1,0:T(8,128)S(1)} %bitcast.24, f32[256,128]{1,0:T(8,128)S(1)} %get-tuple-element.45.sum_ref, f32[256,128]{1,0:T(8,128)S(1)} %get-tuple-element.46.normed_two_ref, ...), custom_call_target="tpu_custom_call" | custom-call | tf_op jit(solution)/shard_map/pallas_call | solution.py:743
  51.8 0.1 collective-permute-start
  51.8 0.5 shard_map.114
  52.4 0.8 %collective-permute-done.got_ref = f32[288,128]{1,0:T(8,128)S(1)} collective-permute-done((f32[288,128]{1,0:T(8,128)S(1)}, f32[288,128]{1,0:T(8,128)S(1)}, u32[]{:S(2)}, u32[]{:S(2)}) %collective-permute-start) | collective-permute-done | bytes 147488 | tf_op jit(solution)/shard_map/ppermute | solution.py:748
  53.2 10.6 %all_to_all.34 = f32[32,1,1280]{2,1,0:T(1,128)S(1)} all-to-all(f32[32,1,1280]{2,1,0:T(1,128)S(1)} %bitcast.29), channel_id=1, replica_groups=mesh['row'=8,'col'=4] {'row','col'}, dimensions={0} | all-to-all | bytes 327680 | tf_op jit(solution)/shard_map/all_to_all | solution.py:709
  63.8 0.5 shard_map.116
  64.3 12.2 %all_to_all.35 = f32[32,1,2176]{2,1,0:T(1,128)S(1)} all-to-all(f32[32,1,2176]{2,1,0:T(1,128)S(1)} %bitcast.30), channel_id=1, replica_groups=mesh['row'=8,'col'=4] {'row','col'}, dimensions={0} | all-to-all | bytes 557056 | tf_op jit(solution)/shard_map/all_to_all | solution.py:709
  76.5 0.4 collective-permute-start.1
  76.9 0.9 %shard_map.117 = (f32[16,2048]{1,0:T(8,128)}, f32[16,2048]{1,0:T(8,128)}, f32[2,64]{1,0:T(2,128)}, f32[2,64]{1,0:T(2,128)}) custom-call(f32[288,128]{1,0:T(8,128)S(1)} %bitcast.25, f32[544,128]{1,0:T(8,128)S(1)} %bitcast.20, f32[1,128]{1,0:T(1,128)S(1)} %get-tuple-element.60.total_one_ref, f32[1,128]{1,0:T(1,128)S(1)} %get-tuple-element.61.total_two_ref), custom_call_target="tpu_custom_call" | custom-call | flops 4194304 | bytes 4194304 | tf_op jit(solution)/shard_map/pallas_call | solution.py:766
  77.8 0.3 collective-permute-done.1.partner_ref
  78.1 1.0 %shard_map.118 = (f32[9,64,64]{2,1,0:T(8,128)}, f32[9,64,64]{2,1,0:T(8,128)}) custom-call(f32[544,128]{1,0:T(8,128)S(1)} %bitcast.21, f32[544,128]{1,0:T(8,128)S(1)} %collective-permute-done.1.partner_ref), custom_call_target="tpu_custom_call" | custom-call | tf_op jit(solution)/shard_map/pallas_call | solution.py:772
  (1 shorter events, 0.0 us)
Async XLA Ops:
  0.6 16.8 %copy-start = (f32[3,3,64,64]{3,2,1,0:T(8,128)S(1)}, f32[3,3,64,64]{3,2,1,0:T(8,128)}, u32[]{:S(2)}) copy-start(f32[3,3,64,64]{3,2,1,0:T(8,128)} %weight_ref.7) | copy-start | bytes 442372
  17.4 11.0 %copy-start.1 = (f32[3,3,64,64]{3,2,1,0:T(8,128)S(1)}, f32[3,3,64,64]{3,2,1,0:T(8,128)}, u32[]{:S(2)}) copy-start(f32[3,3,64,64]{3,2,1,0:T(8,128)} %weight_ref.6) | copy-start | bytes 442372
  51.8 1.4 %collective-permute-start = (f32[288,128]{1,0:T(8,128)S(1)}, f32[288,128]{1,0:T(8,128)S(1)}, u32[]{:S(2)}, u32[]{:S(2)}) collective-permute-start(f32[288,128]{1,0:T(8,128)S(1)} %get-tuple-element.53), channel_id=1, source_target_pairs={{0,4},{4,0},{8,12},{12,8},{16,20},{20,16},{24,28},{28,24},{1,5},{5... | collective-permute-start | bytes 442376 | tf_op jit(solution)/shard_map/ppermute | solution.py:748
  76.5 1.6 %collective-permute-start.1 = (f32[544,128]{1,0:T(8,128)S(1)}, f32[544,128]{1,0:T(8,128)S(1)}, u32[]{:S(2)}, u32[]{:S(2)}) collective-permute-start(f32[544,128]{1,0:T(8,128)S(1)} %bitcast.19), channel_id=1, source_target_pairs={{0,4},{4,0},{8,12},{12,8},{16,20},{20,16},{24,28},{28,24},{1,5},{5... | collective-permute-start | bytes 835592 | tf_op jit(solution)/shard_map/ppermute | solution.py:765

commit v7 on v6

--- a/solution.py
+++ b/solution.py
@@ -663,10 +663,35 @@
         send_ref[begin + SLOTS : begin + stride, :] = two if owner_core(d) else one
 
 
+def pick_kernel(devices, share, recv_ref, rows_ref):
+    for d in range(devices):
+        begin = d * (share + SLOTS) + SLOTS
+        rows_ref[d * share : (d + 1) * share, :] = recv_ref[begin : begin + share, :]
+
+
+def write_taps(rows_ref, taps_ref, first, one_ref, two_ref, sem):
+    for tap in range(9):
+        block = rows_ref[tap * HALF // 2 : (tap + 1) * HALF // 2, :]
+        taps_ref[tap, : HALF // 2, :] = block[:, :HALF]
+        taps_ref[tap, HALF // 2 :, :] = swap_halves(block)[:, :HALF]
+
+    @pl.when(first)
+    def _():
+        pltpu.make_async_copy(taps_ref, one_ref, sem).start()
+
+    @pl.when(jnp.logical_not(first))
+    def _():
+        pltpu.make_async_copy(taps_ref, two_ref, sem).start()
+
+    return pltpu.make_async_copy(taps_ref, one_ref, sem)
+
+
 def map_kernel(
-    table, share, residues, sym_recv_ref, recv_ref, total_one_ref, total_two_ref,
-    sym_ref, map_ref, gain_ref, shift_ref, scratch_ref, other_ref,
+    table, share, residues, sym_recv_ref, recv_ref, rows_ref, total_one_ref, total_two_ref,
+    sym_ref, map_ref, gain_ref, shift_ref, one_ref, two_ref,
+    scratch_ref, other_ref, taps_ref, sem,
 ):
+    copy = write_taps(rows_ref, taps_ref, first_core(), one_ref, two_ref, sem)
     unpack_rows(table, sym_recv_ref, scratch_ref, SLOTS + 1, 0)
     join_phases(scratch_ref, sym_ref)
     unpack_rows(table, recv_ref, other_ref, share + SLOTS, 0)
@@ -675,23 +700,14 @@
         total = total_ref[...] / residues
         shift_ref[index : index + 1, :] = total[:, :HALF]
         gain_ref[index : index + 1, :] = swap_halves(total)[:, :HALF]
-
-
-def grad_kernel(devices, share, mine_ref, partner_ref, one_ref, two_ref, first_ref, second_ref):
-    stride = share + SLOTS
-    for source_ref, rows_ref in ((mine_ref, first_ref), (partner_ref, second_ref)):
-        for d in range(devices):
-            begin = d * stride + SLOTS
-            rows_ref[d * share : (d + 1) * share, :] = source_ref[begin : begin + share, :]
-    even = first_core()
-    for tap in range(9):
-        begin = tap * HALF // 2
-        mine = first_ref[begin : begin + HALF // 2, :]
-        partner = second_ref[begin : begin + HALF // 2, :]
-        one, two = jnp.where(even, mine, partner), jnp.where(even, partner, mine)
-        for block, out_ref in ((one, one_ref), (two, two_ref)):
-            out_ref[tap, : HALF // 2, :] = block[:, :HALF]
-            out_ref[tap, HALF // 2 :, :] = swap_halves(block)[:, :HALF]
+    copy.wait()
+
+
+def grad_kernel(rows_ref, own_one_ref, own_two_ref, one_ref, two_ref, taps_ref, sem):
+    del own_one_ref, own_two_ref
+    write_taps(
+        rows_ref, taps_ref, jnp.logical_not(first_core()), one_ref, two_ref, sem
+    ).wait()
 
 
 def call(body, shapes, scratch=(), cost=None):
@@ -762,16 +778,34 @@
     )
     recv = exchange(send, devices)
     taps = conv_one.shape[0] * conv_one.shape[1]
-    partner = lax.ppermute(recv, "row", cores)
-    sym_out, grad_map, grad_gain, grad_shift = call(
+    (collected,) = call(part(pick_kernel, devices, share), [rows])(recv)
+    partner = lax.ppermute(collected, "row", cores)
+    blocks = jax.ShapeDtypeStruct((taps, HALF, HALF), jnp.float32)
+    in_vmem = pl.BlockSpec(memory_space=pltpu.VMEM)
+    in_hbm = pl.BlockSpec(memory_space=pl.ANY)
+    taps_scratch = [pltpu.VMEM(blocks.shape, jnp.float32), pltpu.SemaphoreType.DMA]
+    params = pltpu.CompilerParams(vmem_limit_bytes=VMEM_BYTES)
+    sym_out, grad_map, grad_gain, grad_shift, own_one, own_two = pl.pallas_call(
         part(map_kernel, table, share, residues),
-        [pair_map.shape, pair_map.shape, norm_gain.shape, norm_shift.shape],
-        [whole, whole],
-        cost,
-    )(sym_recv, recv, total_one, total_two)
-    grad_one, grad_two = call(
-        part(grad_kernel, devices, share), [(taps, HALF, HALF)] * 2, [rows, rows]
-    )(recv, partner)
+        out_shape=[
+            jax.ShapeDtypeStruct(v.shape, jnp.float32)
+            for v in (pair_map, pair_map, norm_gain, norm_shift)
+        ]
+        + [blocks] * 2,
+        out_specs=[in_vmem] * 4 + [in_hbm] * 2,
+        scratch_shapes=[pltpu.VMEM(whole, jnp.float32)] * 2 + taps_scratch,
+        compiler_params=params,
+        cost_estimate=cost,
+    )(sym_recv, recv, collected, total_one, total_two)
+    grad_one, grad_two = pl.pallas_call(
+        grad_kernel,
+        out_shape=[blocks] * 2,
+        in_specs=[in_vmem] + [in_hbm] * 2,
+        out_specs=[in_hbm] * 2,
+        input_output_aliases={1: 0, 2: 1},
+        scratch_shapes=taps_scratch,
+        compiler_params=params,
+    )(partner, own_one, own_two)
     return (
         sym_out,
         grad_map,

time: 79.3 us -> 79.7 us (level)
    pallas_call x2 -> x3, Pallas kernels: 1.89 us -> 2.44 us  [the longest x1 1.59 us: phase_body(): pl.pallas_call(part(map_kernel, table, share, residues), out_shape=[jax.S...]
  transfers between devices with their start and end apart: 2 -> 2, of which waited for: 2 -> 1; matrix products, arithmetic and copies ran while one was open for 0% -> 0% of each run, Pallas kernels for 2% -> 3%
where the time goes in v7:
time: 79.7 us; the launch traced here: 79.4 us
  blocking collectives  69.8 us (88%)
  Pallas kernels  7.46 us (9%)
  waiting for transfers between devices  0.82 us (1%)
    all_to_all x6, blocking collectives, exchange(): lax.all_to_all(sent, AXES, split_axis=0, concat_axis=0, tiled=True)  69.8 us
  transfers between devices with their start and end apart: 2, of which 1 were waited for; matrix products, arithmetic and copies ran while one was open for 0% of the time, Pallas kernels for 3%

profile of v7, /device:TPU:0, one launch (start us, length us, event | category | flops | bytes accessed | tf_op | source)
XLA Modules:
  0.0 79.4 jit_solution(3631583456928119066)
XLA Ops:
  0.6 0.0 copy-start
  0.6 1.2 %shard_map.109 = (f32[256,128]{1,0:T(8,128)S(1)}, f32[256,128]{1,0:T(8,128)S(1)}, f32[8,128]{1,0:T(8,128)S(1)}) custom-call(f32[16,2048]{1,0:T(8,128)} %x_ref.1, f32[16,2048]{1,0:T(8,128)} %g_ref.1, f32[2,64]{1,0:T(2,128)} %gain_ref.1, f32[2,64]{1,0:T(2,128)} %shift_ref.1), custom_call_target="tpu_custom_call" | custom-call | tf_op jit(solution)/shard_map/pallas_call | solution.py:741
  1.9 15.5 %all_to_all.30 = f32[32,1,1024]{2,1,0:T(1,128)S(1)} all-to-all(f32[32,1,1024]{2,1,0:T(1,128)S(1)} %bitcast.33), channel_id=1, replica_groups=mesh['row'=8,'col'=4] {'row','col'}, dimensions={0} | all-to-all | bytes 262144 | tf_op jit(solution)/shard_map/all_to_all | solution.py:725
  17.4 0.0 copy-done
  17.4 0.0 copy-start.1
  17.4 0.7 shard_map.110
  18.1 10.3 %all_to_all.31 = f32[32,1,1152]{2,1,0:T(1,128)S(1)} all-to-all(f32[32,1,1152]{2,1,0:T(1,128)S(1)} %bitcast.32), channel_id=1, replica_groups=mesh['row'=8,'col'=4] {'row','col'}, dimensions={0} | all-to-all | bytes 294912 | tf_op jit(solution)/shard_map/all_to_all | solution.py:725
  28.4 0.0 copy-done.1
  28.4 0.9 %shard_map.111 = (f32[256,128]{1,0:T(8,128)S(1)}, f32[1,128]{1,0:T(1,128)S(1)}, f32[256,128]{1,0:T(8,128)S(1)}, f32[256,128]{1,0:T(8,128)S(1)}, f32[352,128]{1,0:T(8,128)S(1)}) custom-call(f32[288,128]{1,0:T(8,128)S(1)} %bitcast.25, f32[256,128]{1,0:T(8,128)S(1)} %get-tuple-element.42.hidden_ref, f32[256,128]{1,0:T(8,128)S(1)} %bitcast.15, ...), custom_call_target="tpu_custom_call" | custom-call | tf_op jit(solution)/shard_map/pallas_call | solution.py:749
  29.3 10.8 %all_to_all.32 = f32[32,1,1408]{2,1,0:T(1,128)S(1)} all-to-all(f32[32,1,1408]{2,1,0:T(1,128)S(1)} %bitcast.30), channel_id=1, replica_groups=mesh['row'=8,'col'=4] {'row','col'}, dimensions={0} | all-to-all | bytes 360448 | tf_op jit(solution)/shard_map/all_to_all | solution.py:725
  40.0 0.3 shard_map.112
  40.3 10.5 %all_to_all.33 = f32[32,1,1152]{2,1,0:T(1,128)S(1)} all-to-all(f32[32,1,1152]{2,1,0:T(1,128)S(1)} %bitcast.31), channel_id=1, replica_groups=mesh['row'=8,'col'=4] {'row','col'}, dimensions={0} | all-to-all | bytes 294912 | tf_op jit(solution)/shard_map/all_to_all | solution.py:725
  50.8 1.0 %shard_map.113 = (f32[256,128]{1,0:T(8,128)S(1)}, f32[1,128]{1,0:T(1,128)S(1)}, f32[1,128]{1,0:T(1,128)S(1)}, f32[256,128]{1,0:T(8,128)S(1)}, f32[288,128]{1,0:T(8,128)S(1)}) custom-call(f32[288,128]{1,0:T(8,128)S(1)} %bitcast.23, f32[256,128]{1,0:T(8,128)S(1)} %get-tuple-element.47.sum_ref, f32[256,128]{1,0:T(8,128)S(1)} %get-tuple-element.48.normed_two_ref, ...), custom_call_target="tpu_custom_call" | custom-call | tf_op jit(solution)/shard_map/pallas_call | solution.py:759
  51.8 0.1 collective-permute-start
  51.8 0.5 shard_map.114
  52.4 0.8 %collective-permute-done.got_ref = f32[288,128]{1,0:T(8,128)S(1)} collective-permute-done((f32[288,128]{1,0:T(8,128)S(1)}, f32[288,128]{1,0:T(8,128)S(1)}, u32[]{:S(2)}, u32[]{:S(2)}) %collective-permute-start) | collective-permute-done | bytes 147488 | tf_op jit(solution)/shard_map/ppermute | solution.py:764
  53.2 10.6 %all_to_all.34 = f32[32,1,1280]{2,1,0:T(1,128)S(1)} all-to-all(f32[32,1,1280]{2,1,0:T(1,128)S(1)} %bitcast.28), channel_id=1, replica_groups=mesh['row'=8,'col'=4] {'row','col'}, dimensions={0} | all-to-all | bytes 327680 | tf_op jit(solution)/shard_map/all_to_all | solution.py:725
  63.8 0.5 shard_map.116
  64.3 12.2 %all_to_all.35 = f32[32,1,2176]{2,1,0:T(1,128)S(1)} all-to-all(f32[32,1,2176]{2,1,0:T(1,128)S(1)} %bitcast.29), channel_id=1, replica_groups=mesh['row'=8,'col'=4] {'row','col'}, dimensions={0} | all-to-all | bytes 557056 | tf_op jit(solution)/shard_map/all_to_all | solution.py:725
  76.5 0.5 collective-permute-start.1
  77.0 1.6 %shard_map.118 = (f32[16,2048]{1,0:T(8,128)}, f32[16,2048]{1,0:T(8,128)}, f32[2,64]{1,0:T(2,128)}, f32[2,64]{1,0:T(2,128)}, f32[9,64,64]{2,1,0:T(8,128)}, /*index=5*/f32[9,64,64]{2,1,0:T(8,128)}) custom-call(f32[288,128]{1,0:T(8,128)S(1)} %bitcast.24, f32[544,128]{1,0:T(8,128)S(1)} %bitcast.20, f32[288,128]{1,0:T(8,128)S(1)} %shard_map.117.rows_ref, ...), custom_call_target="tpu_custom_call" | custom-call | flops 4194304 | bytes 4194304 | tf_op jit(solution)/shard_map/pallas_call | solution.py:788
  78.6 0.0 collective-permute-done.1.rows_ref
  78.6 0.8 %shard_map.119 = (f32[9,64,64]{2,1,0:T(8,128)}, f32[9,64,64]{2,1,0:T(8,128)}) custom-call(f32[288,128]{1,0:T(8,128)S(1)} %collective-permute-done.1.rows_ref, f32[9,64,64]{2,1,0:T(8,128)} %get-tuple-element.66.own_one_ref, f32[9,64,64]{2,1,0:T(8,128)} %get-tuple-element.67.own_two_ref), custom_call_target="tpu_custom_call", output_to_operand_aliasing={{0}: (1, {}), {1}: (2, {})} | custom-call | tf_op jit(solution)/shard_map/pallas_call | solution.py:800
  (2 shorter events, 0.1 us)
Async XLA Ops:
  0.6 16.8 %copy-start = (f32[3,3,64,64]{3,2,1,0:T(8,128)S(1)}, f32[3,3,64,64]{3,2,1,0:T(8,128)}, u32[]{:S(2)}) copy-start(f32[3,3,64,64]{3,2,1,0:T(8,128)} %weight_ref.7) | copy-start | bytes 442372
  17.4 11.0 %copy-start.1 = (f32[3,3,64,64]{3,2,1,0:T(8,128)S(1)}, f32[3,3,64,64]{3,2,1,0:T(8,128)}, u32[]{:S(2)}) copy-start(f32[3,3,64,64]{3,2,1,0:T(8,128)} %weight_ref.6) | copy-start | bytes 442372
  51.8 1.4 %collective-permute-start = (f32[288,128]{1,0:T(8,128)S(1)}, f32[288,128]{1,0:T(8,128)S(1)}, u32[]{:S(2)}, u32[]{:S(2)}) collective-permute-start(f32[288,128]{1,0:T(8,128)S(1)} %get-tuple-element.55), channel_id=1, source_target_pairs={{0,4},{4,0},{8,12},{12,8},{16,20},{20,16},{24,28},{28,24},{1,5},{5... | collective-permute-start | bytes 442376 | tf_op jit(solution)/shard_map/ppermute | solution.py:764
  76.5 2.1 %collective-permute-start.1 = (f32[288,128]{1,0:T(8,128)S(1)}, f32[288,128]{1,0:T(8,128)S(1)}, u32[]{:S(2)}, u32[]{:S(2)}) collective-permute-start(f32[288,128]{1,0:T(8,128)S(1)} %shard_map.117.rows_ref), channel_id=1, source_target_pairs={{0,4},{4,0},{8,12},{12,8},{16,20},{20,16},{24,28},{28,24},{1,5},{5... | collective-permute-start | bytes 442376 | tf_op jit(solution)/shard_map/ppermute | solution.py:782

commit v8 on v7

--- a/solution.py
+++ b/solution.py
@@ -669,45 +669,54 @@
         rows_ref[d * share : (d + 1) * share, :] = recv_ref[begin : begin + share, :]
 
 
-def write_taps(rows_ref, taps_ref, first, one_ref, two_ref, sem):
-    for tap in range(9):
-        block = rows_ref[tap * HALF // 2 : (tap + 1) * HALF // 2, :]
-        taps_ref[tap, : HALF // 2, :] = block[:, :HALF]
-        taps_ref[tap, HALF // 2 :, :] = swap_halves(block)[:, :HALF]
-
-    @pl.when(first)
-    def _():
-        pltpu.make_async_copy(taps_ref, one_ref, sem).start()
-
-    @pl.when(jnp.logical_not(first))
-    def _():
-        pltpu.make_async_copy(taps_ref, two_ref, sem).start()
-
-    return pltpu.make_async_copy(taps_ref, one_ref, sem)
+def write_taps(rows_ref, taps_ref, first, one_ref, two_ref, sems):
+    copies = []
+    for a in range(3):
+        part = pl.ds(3 * a, 3)
+        for tap in range(3 * a, 3 * a + 3):
+            block = rows_ref[tap * HALF // 2 : (tap + 1) * HALF // 2, :]
+            taps_ref[tap, : HALF // 2, :] = block[:, :HALF]
+            taps_ref[tap, HALF // 2 :, :] = swap_halves(block)[:, :HALF]
+        to_one = pltpu.make_async_copy(taps_ref.at[part], one_ref.at[part], sems.at[a])
+        to_two = pltpu.make_async_copy(taps_ref.at[part], two_ref.at[part], sems.at[a])
+        pl.when(first)(to_one.start)
+        pl.when(jnp.logical_not(first))(to_two.start)
+        copies.append(to_one)
+    return copies
 
 
 def map_kernel(
     table, share, residues, sym_recv_ref, recv_ref, rows_ref, total_one_ref, total_two_ref,
-    sym_ref, map_ref, gain_ref, shift_ref, one_ref, two_ref,
-    scratch_ref, other_ref, taps_ref, sem,
+    gain_ref, shift_ref, sym_ref, map_ref, one_ref, two_ref,
+    scratch_ref, other_ref, gains_ref, shifts_ref, sym_tile_ref, map_tile_ref, taps_ref,
+    tile_sems, sems,
 ):
-    copy = write_taps(rows_ref, taps_ref, first_core(), one_ref, two_ref, sem)
-    unpack_rows(table, sym_recv_ref, scratch_ref, SLOTS + 1, 0)
-    join_phases(scratch_ref, sym_ref)
-    unpack_rows(table, recv_ref, other_ref, share + SLOTS, 0)
-    join_phases(other_ref, map_ref)
+    copies = write_taps(rows_ref, taps_ref, first_core(), one_ref, two_ref, sems)
     for index, total_ref in ((0, total_one_ref), (1, total_two_ref)):
         total = total_ref[...] / residues
-        shift_ref[index : index + 1, :] = total[:, :HALF]
-        gain_ref[index : index + 1, :] = swap_halves(total)[:, :HALF]
-    copy.wait()
-
-
-def grad_kernel(rows_ref, own_one_ref, own_two_ref, one_ref, two_ref, taps_ref, sem):
+        shifts_ref[index : index + 1, :] = total[:, :HALF]
+        gains_ref[index : index + 1, :] = swap_halves(total)[:, :HALF]
+    copies.append(pltpu.make_async_copy(gains_ref, gain_ref, tile_sems.at[2]))
+    copies[-1].start()
+    copies.append(pltpu.make_async_copy(shifts_ref, shift_ref, tile_sems.at[3]))
+    copies[-1].start()
+    unpack_rows(table, sym_recv_ref, scratch_ref, SLOTS + 1, 0)
+    join_phases(scratch_ref, sym_tile_ref)
+    copies.append(pltpu.make_async_copy(sym_tile_ref, sym_ref, tile_sems.at[0]))
+    copies[-1].start()
+    unpack_rows(table, recv_ref, other_ref, share + SLOTS, 0)
+    join_phases(other_ref, map_tile_ref)
+    copies.append(pltpu.make_async_copy(map_tile_ref, map_ref, tile_sems.at[1]))
+    copies[-1].start()
+    for copy in copies:
+        copy.wait()
+
+
+def grad_kernel(rows_ref, own_one_ref, own_two_ref, one_ref, two_ref, taps_ref, sems):
     del own_one_ref, own_two_ref
-    write_taps(
-        rows_ref, taps_ref, jnp.logical_not(first_core()), one_ref, two_ref, sem
-    ).wait()
+    second = jnp.logical_not(first_core())
+    for copy in write_taps(rows_ref, taps_ref, second, one_ref, two_ref, sems):
+        copy.wait()
 
 
 def call(body, shapes, scratch=(), cost=None):
@@ -783,17 +792,19 @@
     blocks = jax.ShapeDtypeStruct((taps, HALF, HALF), jnp.float32)
     in_vmem = pl.BlockSpec(memory_space=pltpu.VMEM)
     in_hbm = pl.BlockSpec(memory_space=pl.ANY)
-    taps_scratch = [pltpu.VMEM(blocks.shape, jnp.float32), pltpu.SemaphoreType.DMA]
+    taps_scratch = [pltpu.VMEM(blocks.shape, jnp.float32), pltpu.SemaphoreType.DMA((3,))]
     params = pltpu.CompilerParams(vmem_limit_bytes=VMEM_BYTES)
-    sym_out, grad_map, grad_gain, grad_shift, own_one, own_two = pl.pallas_call(
+    outs = (norm_gain, norm_shift, pair_map, pair_map)
+    tiles = [pltpu.VMEM(v.shape, jnp.float32) for v in outs]
+    grad_gain, grad_shift, sym_out, grad_map, own_one, own_two = pl.pallas_call(
         part(map_kernel, table, share, residues),
-        out_shape=[
-            jax.ShapeDtypeStruct(v.shape, jnp.float32)
-            for v in (pair_map, pair_map, norm_gain, norm_shift)
-        ]
-        + [blocks] * 2,
-        out_specs=[in_vmem] * 4 + [in_hbm] * 2,
-        scratch_shapes=[pltpu.VMEM(whole, jnp.float32)] * 2 + taps_scratch,
+        out_shape=[jax.ShapeDtypeStruct(v.shape, jnp.float32) for v in outs] + [blocks] * 2,
+        out_specs=[in_hbm] * 6,
+        scratch_shapes=[pltpu.VMEM(whole, jnp.float32)] * 2
+        + tiles
+        + taps_scratch[:1]
+        + [pltpu.SemaphoreType.DMA((4,))]
+        + taps_scratch[1:],
         compiler_params=params,
         cost_estimate=cost,
     )(sym_recv, recv, collected, total_one, total_two)

time: 79.7 us -> 79.1 us (level)
  transfers between devices with their start and end apart: 2 -> 2, of which waited for: 1 -> 1; matrix products, arithmetic and copies ran while one was open for 0% -> 0% of each run, Pallas kernels for 3% -> 2%
where the time goes in v8:
time: 79.1 us; the launch traced here: 78.8 us
  blocking collectives  69.8 us (88%)
  Pallas kernels  6.85 us (9%)
  waiting for transfers between devices  0.82 us (1%)
    all_to_all x6, blocking collectives, exchange(): lax.all_to_all(sent, AXES, split_axis=0, concat_axis=0, tiled=True)  69.8 us
  transfers between devices with their start and end apart: 2, of which 1 were waited for; matrix products, arithmetic and copies ran while one was open for 0% of the time, Pallas kernels for 2%

profile of v8, /device:TPU:0, one launch (start us, length us, event | category | flops | bytes accessed | tf_op | source)
XLA Modules:
  0.0 78.8 jit_solution(17382721492797604411)
XLA Ops:
  0.6 0.0 copy-start
  0.6 1.2 %shard_map.109 = (f32[256,128]{1,0:T(8,128)S(1)}, f32[256,128]{1,0:T(8,128)S(1)}, f32[8,128]{1,0:T(8,128)S(1)}) custom-call(f32[16,2048]{1,0:T(8,128)} %x_ref.1, f32[16,2048]{1,0:T(8,128)} %g_ref.1, f32[2,64]{1,0:T(2,128)} %gain_ref.1, f32[2,64]{1,0:T(2,128)} %shift_ref.1), custom_call_target="tpu_custom_call" | custom-call | tf_op jit(solution)/shard_map/pallas_call | solution.py:750
  1.9 15.5 %all_to_all.30 = f32[32,1,1024]{2,1,0:T(1,128)S(1)} all-to-all(f32[32,1,1024]{2,1,0:T(1,128)S(1)} %bitcast.33), channel_id=1, replica_groups=mesh['row'=8,'col'=4] {'row','col'}, dimensions={0} | all-to-all | bytes 262144 | tf_op jit(solution)/shard_map/all_to_all | solution.py:734
  17.4 0.0 copy-done
  17.4 0.0 copy-start.1
  17.4 0.7 shard_map.110
  18.1 10.3 %all_to_all.31 = f32[32,1,1152]{2,1,0:T(1,128)S(1)} all-to-all(f32[32,1,1152]{2,1,0:T(1,128)S(1)} %bitcast.32), channel_id=1, replica_groups=mesh['row'=8,'col'=4] {'row','col'}, dimensions={0} | all-to-all | bytes 294912 | tf_op jit(solution)/shard_map/all_to_all | solution.py:734
  28.4 0.0 copy-done.1
  28.4 0.9 %shard_map.111 = (f32[256,128]{1,0:T(8,128)S(1)}, f32[1,128]{1,0:T(1,128)S(1)}, f32[256,128]{1,0:T(8,128)S(1)}, f32[256,128]{1,0:T(8,128)S(1)}, f32[352,128]{1,0:T(8,128)S(1)}) custom-call(f32[288,128]{1,0:T(8,128)S(1)} %bitcast.25, f32[256,128]{1,0:T(8,128)S(1)} %get-tuple-element.42.hidden_ref, f32[256,128]{1,0:T(8,128)S(1)} %bitcast.15, ...), custom_call_target="tpu_custom_call" | custom-call | tf_op jit(solution)/shard_map/pallas_call | solution.py:758
  29.3 10.8 %all_to_all.32 = f32[32,1,1408]{2,1,0:T(1,128)S(1)} all-to-all(f32[32,1,1408]{2,1,0:T(1,128)S(1)} %bitcast.30), channel_id=1, replica_groups=mesh['row'=8,'col'=4] {'row','col'}, dimensions={0} | all-to-all | bytes 360448 | tf_op jit(solution)/shard_map/all_to_all | solution.py:734
  40.0 0.3 shard_map.112
  40.3 10.5 %all_to_all.33 = f32[32,1,1152]{2,1,0:T(1,128)S(1)} all-to-all(f32[32,1,1152]{2,1,0:T(1,128)S(1)} %bitcast.31), channel_id=1, replica_groups=mesh['row'=8,'col'=4] {'row','col'}, dimensions={0} | all-to-all | bytes 294912 | tf_op jit(solution)/shard_map/all_to_all | solution.py:734
  50.8 1.0 %shard_map.113 = (f32[256,128]{1,0:T(8,128)S(1)}, f32[1,128]{1,0:T(1,128)S(1)}, f32[1,128]{1,0:T(1,128)S(1)}, f32[256,128]{1,0:T(8,128)S(1)}, f32[288,128]{1,0:T(8,128)S(1)}) custom-call(f32[288,128]{1,0:T(8,128)S(1)} %bitcast.23, f32[256,128]{1,0:T(8,128)S(1)} %get-tuple-element.47.sum_ref, f32[256,128]{1,0:T(8,128)S(1)} %get-tuple-element.48.normed_two_ref, ...), custom_call_target="tpu_custom_call" | custom-call | tf_op jit(solution)/shard_map/pallas_call | solution.py:768
  51.8 0.1 collective-permute-start
  51.8 0.5 shard_map.114
  52.4 0.8 %collective-permute-done.got_ref = f32[288,128]{1,0:T(8,128)S(1)} collective-permute-done((f32[288,128]{1,0:T(8,128)S(1)}, f32[288,128]{1,0:T(8,128)S(1)}, u32[]{:S(2)}, u32[]{:S(2)}) %collective-permute-start) | collective-permute-done | bytes 147488 | tf_op jit(solution)/shard_map/ppermute | solution.py:773
  53.2 10.6 %all_to_all.34 = f32[32,1,1280]{2,1,0:T(1,128)S(1)} all-to-all(f32[32,1,1280]{2,1,0:T(1,128)S(1)} %bitcast.28), channel_id=1, replica_groups=mesh['row'=8,'col'=4] {'row','col'}, dimensions={0} | all-to-all | bytes 327680 | tf_op jit(solution)/shard_map/all_to_all | solution.py:734
  63.8 0.5 shard_map.116
  64.3 12.2 %all_to_all.35 = f32[32,1,2176]{2,1,0:T(1,128)S(1)} all-to-all(f32[32,1,2176]{2,1,0:T(1,128)S(1)} %bitcast.29), channel_id=1, replica_groups=mesh['row'=8,'col'=4] {'row','col'}, dimensions={0} | all-to-all | bytes 557056 | tf_op jit(solution)/shard_map/all_to_all | solution.py:734
  76.5 0.5 collective-permute-start.1
  77.0 1.0 %shard_map.118 = (f32[2,64]{1,0:T(2,128)}, f32[2,64]{1,0:T(2,128)}, f32[16,2048]{1,0:T(8,128)}, f32[16,2048]{1,0:T(8,128)}, f32[9,64,64]{2,1,0:T(8,128)}, /*index=5*/f32[9,64,64]{2,1,0:T(8,128)}) custom-call(f32[288,128]{1,0:T(8,128)S(1)} %bitcast.24, f32[544,128]{1,0:T(8,128)S(1)} %bitcast.20, f32[288,128]{1,0:T(8,128)S(1)} %shard_map.117.rows_ref, ...), custom_call_target="tpu_custom_call" | custom-call | flops 4194304 | bytes 4194304 | tf_op jit(solution)/shard_map/pallas_call | solution.py:799
  78.0 0.0 collective-permute-done.1.rows_ref
  78.0 0.8 %shard_map.119 = (f32[9,64,64]{2,1,0:T(8,128)}, f32[9,64,64]{2,1,0:T(8,128)}) custom-call(f32[288,128]{1,0:T(8,128)S(1)} %collective-permute-done.1.rows_ref, f32[9,64,64]{2,1,0:T(8,128)} %get-tuple-element.66.own_one_ref, f32[9,64,64]{2,1,0:T(8,128)} %get-tuple-element.67.own_two_ref), custom_call_target="tpu_custom_call", output_to_operand_aliasing={{0}: (1, {}), {1}: (2, {})} | custom-call | tf_op jit(solution)/shard_map/pallas_call | solution.py:811
  (2 shorter events, 0.1 us)
Async XLA Ops:
  0.6 16.8 %copy-start = (f32[3,3,64,64]{3,2,1,0:T(8,128)S(1)}, f32[3,3,64,64]{3,2,1,0:T(8,128)}, u32[]{:S(2)}) copy-start(f32[3,3,64,64]{3,2,1,0:T(8,128)} %weight_ref.7) | copy-start | bytes 442372
  17.4 11.0 %copy-start.1 = (f32[3,3,64,64]{3,2,1,0:T(8,128)S(1)}, f32[3,3,64,64]{3,2,1,0:T(8,128)}, u32[]{:S(2)}) copy-start(f32[3,3,64,64]{3,2,1,0:T(8,128)} %weight_ref.6) | copy-start | bytes 442372
  51.8 1.4 %collective-permute-start = (f32[288,128]{1,0:T(8,128)S(1)}, f32[288,128]{1,0:T(8,128)S(1)}, u32[]{:S(2)}, u32[]{:S(2)}) collective-permute-start(f32[288,128]{1,0:T(8,128)S(1)} %get-tuple-element.55), channel_id=1, source_target_pairs={{0,4},{4,0},{8,12},{12,8},{16,20},{20,16},{24,28},{28,24},{1,5},{5... | collective-permute-start | bytes 442376 | tf_op jit(solution)/shard_map/ppermute | solution.py:773
  76.5 1.5 %collective-permute-start.1 = (f32[288,128]{1,0:T(8,128)S(1)}, f32[288,128]{1,0:T(8,128)S(1)}, u32[]{:S(2)}, u32[]{:S(2)}) collective-permute-start(f32[288,128]{1,0:T(8,128)S(1)} %shard_map.117.rows_ref), channel_id=1, source_target_pairs={{0,4},{4,0},{8,12},{12,8},{16,20},{20,16},{24,28},{28,24},{1,5},{5... | collective-permute-start | bytes 442376 | tf_op jit(solution)/shard_map/ppermute | solution.py:791
